TPU v7x, 128 devices: a whole 4x4x4 slice. The times are simulated.
128 devices in a mesh: grp: 4 (over z), leaf: 32 (over y, x, core).
Axes of the slice: x: 4, y: 4, z: 4, core: 2. Of those that a mesh axis runs over, the one named last changes fastest.
Arguments:
- matrix: bfloat16 [131072, 512], P(('grp', 'leaf')), may hold values from -6 to 6
- leaf_basis: bfloat16 [131072, 512], P(('grp', 'leaf')), may hold values from -0.1875 to 0.1875
- leaf_tri: bfloat16 [128, 512, 512], P(('grp', 'leaf')), may hold values from -1.5 to 1.5, as said below
- inner_basis: bfloat16 [4, 32, 5, 1024, 512], P('grp', 'leaf'), may hold values from -1 to 1, as said below
- inner_tri: bfloat16 [4, 32, 5, 512, 512], P('grp', 'leaf'), may hold values from -1.5 to 1.5, as said below
- outer_basis: bfloat16 [4, 32, 2, 1024, 512], P('grp', 'leaf'), may hold values from -1 to 1, as said below
- outer_tri: bfloat16 [4, 32, 2, 512, 512], P('grp', 'leaf'), may hold values from -1.5 to 1.5, as said below
Outputs:
- reduced: bfloat16 [512, 512], P(None, ('grp', 'leaf'))
Inputs may be any that keep to these rules, and one draw needn't show every extreme that they name: `leaf_tri`: upper triangular; diagonal entries between 0.5 and 1.5. `inner_basis`: equal for all leaves under the same inner node of level l. `inner_tri`: upper triangular, diagonal entries between 0.5 and 1.5; equal for all leaves under the same inner node of level l. `outer_basis`: equal for all leaves under the same outer node of level m. `outer_tri`: upper triangular, diagonal entries between 0.5 and 1.5; equal for all leaves under the same outer node of level m.
All inputs are finite; a program needn't handle non-finite values.
Results may differ from a plain program's by a relative error of at most 0.0045.
Values sent between devices are 32-bit elements; how exact they have to be, the bound alone decides.
No kernel may reach another device: no remote copies, remote signals or barrier semaphores. Data moves between devices by JAX's collectives and lax.ppermute only.
A program may use at most 64 MiB of HBM per device.

v0:
```python
import jax
import jax.numpy as jnp
from jax import lax
from jax.sharding import PartitionSpec as P

contract = (((0,), (0,)), ((), ()))


def partner_2(array, axis, stride):
    return lax.ppermute(array, axis, [(i, i ^ 1 << stride) for i in range(lax.axis_size(axis))])


def leaf_reflect(panel_rows, reflectors, triangle):
    rank_width = triangle.shape[-1]
    projected = lax.dot_general(
        reflectors, panel_rows, contract, preferred_element_type=jnp.float32
    )
    mixing = lax.dot_general(
        triangle.astype(jnp.float32), projected, contract, precision=lax.Precision.HIGHEST
    )
    return panel_rows[:rank_width].astype(jnp.float32) - jnp.dot(
        reflectors[:rank_width].astype(jnp.float32), mixing, precision=lax.Precision.HIGHEST
    )


def node_reflect(panel_rows, reflectors, triangle):
    rank_width = triangle.shape[-1]
    basis = reflectors.astype(jnp.float32)
    projected = lax.dot_general(basis, panel_rows, contract, precision=lax.Precision.HIGHEST)
    mixing = lax.dot_general(
        triangle.astype(jnp.float32), projected, contract, precision=lax.Precision.HIGHEST
    )
    return panel_rows[:rank_width] - jnp.dot(
        basis[:rank_width], mixing, precision=lax.Precision.HIGHEST
    )


def pair_rows(own_rows, partner, parity):
    lower_first = jnp.concatenate([own_rows, partner], axis=0)
    upper_first = jnp.concatenate([partner, own_rows], axis=0)
    return jnp.where(parity == 0, lower_first, upper_first)


def own_block(full, device_pos, device_count):
    block_width = full.shape[1] // device_count
    return lax.dynamic_slice_in_dim(full, device_pos * block_width, block_width, 1)


def per_device(matrix, leaf_basis, leaf_tri, inner_basis, inner_tri, outer_basis, outer_tri):
    summit = leaf_reflect(matrix, leaf_basis, leaf_tri[0])
    inner_levels = lax.axis_size("leaf").bit_length() - 1
    outer_levels = lax.axis_size("grp").bit_length() - 1
    leaf_pos = lax.axis_index("leaf")
    group_pos = lax.axis_index("grp")
    device_count = lax.axis_size("grp") * lax.axis_size("leaf")
    device_pos = group_pos * lax.axis_size("leaf") + leaf_pos
    for height in range(inner_levels):
        partner = partner_2(summit, "leaf", height)
        parity = jnp.right_shift(leaf_pos, height) & 1
        summit = node_reflect(
            pair_rows(summit, partner, parity), inner_basis[0, 0, height], inner_tri[0, 0, height]
        )
    for height in range(outer_levels):
        partner = partner_2(summit, "grp", height)
        parity = jnp.right_shift(group_pos, height) & 1
        summit = node_reflect(
            pair_rows(summit, partner, parity), outer_basis[0, 0, height], outer_tri[0, 0, height]
        )
    return own_block(summit, device_pos, device_count).astype(jnp.bfloat16)


def solution(mesh):
    placed = (
        P(("grp", "leaf"), None),
        P(("grp", "leaf"), None),
        P(("grp", "leaf"), None, None),
        P("grp", "leaf", None, None, None),
        P("grp", "leaf", None, None, None),
        P("grp", "leaf", None, None, None),
        P("grp", "leaf", None, None, None),
    )
    return jax.shard_map(
        per_device, mesh=mesh, in_specs=placed, out_specs=P(None, ("grp", "leaf")), check_vma=False
    )
```

profile of v0, /device:TPU:0, one launch (start us, length us, event | category | flops | bytes accessed | tf_op | source)
XLA Modules:
  0.0 206.3 jit_solution(10140489712997665128)
XLA Ops:
  0.0 2.4 %fusion.73 = f32[512,512]{1,0:T(8,128)S(1)} fusion(bf16[1024,512]{1,0:T(8,128)(2,1)} %param.8, bf16[1024,512]{1,0:T(8,128)(2,1)} %param.7), kind=kOutput, calls=%fused_computation.83 | convolution fusion | flops 536870912 | bytes 3145728 | tf_op jit(solution)/shard_map/dot_general | solution.py:15
  2.4 0.2 copy.25
  2.6 1.0 fusion.55
  3.6 0.2 copy-done.5
  3.8 1.0 fusion
  5.0 2.6 %collective-permute-done = f32[512,512]{0,1:T(8,128)S(1)} collective-permute-done((f32[512,512]{0,1:T(8,128)S(1)}, f32[512,512]{0,1:T(8,128)S(1)}, u32[]{:S(2)}, u32[]{:S(2)}) %collective-permute-start) | collective-permute-done | bytes 1048608 | tf_op jit(solution)/shard_map/ppermute | solution.py:10
  7.6 0.4 maximum_select_fusion
  8.0 3.0 %fusion.13 = f32[512,512]{1,0:T(8,128)S(1)} fusion(f32[1024,512]{0,1:T(8,128)S(1)} %maximum_select_fusion, bf16[1,1,5,1024,512]{4,3,2,1,0:T(8,128)(2,1)} %param.10), kind=kOutput, calls=%fused_computation.34 | convolution fusion | flops 3221225472 | bytes 4194304 | tf_op jit(solution)/shard_map/dot_general | solution.py:29
  11.0 2.0 fusion.53
  13.1 2.1 slice_subtract_fusion.5
  15.1 1.7 collective-permute-start.1
  16.8 23.6 %collective-permute-done.1 = f32[512,512]{0,1:T(8,128)S(1)} collective-permute-done((f32[512,512]{0,1:T(8,128)S(1)}, f32[512,512]{0,1:T(8,128)S(1)}, u32[]{:S(2)}, u32[]{:S(2)}) %collective-permute-start.1) | collective-permute-done | bytes 1048608 | tf_op jit(solution)/shard_map/ppermute | solution.py:10
  40.4 0.4 maximum_select_fusion.1
  40.8 3.0 %fusion.11 = f32[512,512]{1,0:T(8,128)S(1)} fusion(f32[1024,512]{0,1:T(8,128)S(1)} %maximum_select_fusion.1, bf16[1,1,5,1024,512]{4,3,2,1,0:T(8,128)(2,1)} %param.10), kind=kOutput, calls=%fused_computation.32 | convolution fusion | flops 3221225472 | bytes 4194304 | tf_op jit(solution)/shard_map/dot_general | solution.py:29
  43.9 2.0 fusion.48
  45.9 2.1 %slice_subtract_fusion.4 = f32[512,512]{0,1:T(8,128)S(1)} fusion(f32[1024,512]{0,1:T(8,128)S(1)} %maximum_select_fusion.1, f32[512,512]{1,0:T(8,128)S(1)} %fusion.48, bf16[1,1,5,1024,512]{4,3,2,1,0:T(8,128)(2,1)} %param.10), kind=kOutput, calls=%fused_computation.20 | convolution fusion | flops 1610874880 | bytes 3670016 | tf_op jit(solution)/shard_map/dot_general | solution.py:33
  48.0 3.3 %collective-permute-start.2 = (f32[512,512]{0,1:T(8,128)S(1)}, f32[512,512]{0,1:T(8,128)S(1)}, u32[]{:S(2)}, u32[]{:S(2)}) collective-permute-start(f32[512,512]{0,1:T(8,128)S(1)} %slice_subtract_fusion.4), channel_id=1, source_target_pairs={{0,4},{1,5},{2,6},{3,7},{4,0},{5,1},{6,2},{7,3},{8,12},{9,13},{10,... | collective-permute-start | bytes 3145736 | tf_op jit(solution)/shard_map/ppermute | solution.py:10
  51.3 22.8 %collective-permute-done.2 = f32[512,512]{0,1:T(8,128)S(1)} collective-permute-done((f32[512,512]{0,1:T(8,128)S(1)}, f32[512,512]{0,1:T(8,128)S(1)}, u32[]{:S(2)}, u32[]{:S(2)}) %collective-permute-start.2) | collective-permute-done | bytes 1048608 | tf_op jit(solution)/shard_map/ppermute | solution.py:10
  74.1 0.4 maximum_select_fusion.2
  74.5 3.0 %fusion.9 = f32[512,512]{1,0:T(8,128)S(1)} fusion(f32[1024,512]{0,1:T(8,128)S(1)} %maximum_select_fusion.2, bf16[1,1,5,1024,512]{4,3,2,1,0:T(8,128)(2,1)} %param.10), kind=kOutput, calls=%fused_computation.30 | convolution fusion | flops 3221225472 | bytes 4194304 | tf_op jit(solution)/shard_map/dot_general | solution.py:29
  77.5 2.0 fusion.43
  79.6 2.1 %slice_subtract_fusion.3 = f32[512,512]{0,1:T(8,128)S(1)} fusion(f32[1024,512]{0,1:T(8,128)S(1)} %maximum_select_fusion.2, f32[512,512]{1,0:T(8,128)S(1)} %fusion.43, bf16[1,1,5,1024,512]{4,3,2,1,0:T(8,128)(2,1)} %param.10), kind=kOutput, calls=%fused_computation.19 | convolution fusion | flops 1610874880 | bytes 3670016 | tf_op jit(solution)/shard_map/dot_general | solution.py:33
  81.7 1.7 collective-permute-start.3
  83.4 21.8 %collective-permute-done.3 = f32[512,512]{0,1:T(8,128)S(1)} collective-permute-done((f32[512,512]{0,1:T(8,128)S(1)}, f32[512,512]{0,1:T(8,128)S(1)}, u32[]{:S(2)}, u32[]{:S(2)}) %collective-permute-start.3) | collective-permute-done | bytes 1048608 | tf_op jit(solution)/shard_map/ppermute | solution.py:10
  105.2 0.4 maximum_select_fusion.3
  105.6 3.0 %fusion.7 = f32[512,512]{1,0:T(8,128)S(1)} fusion(f32[1024,512]{0,1:T(8,128)S(1)} %maximum_select_fusion.3, bf16[1,1,5,1024,512]{4,3,2,1,0:T(8,128)(2,1)} %param.10), kind=kOutput, calls=%fused_computation.28 | convolution fusion | flops 3221225472 | bytes 4194304 | tf_op jit(solution)/shard_map/dot_general | solution.py:29
  108.6 2.0 fusion.38
  110.7 2.1 slice_subtract_fusion.2
  112.7 3.3 %collective-permute-start.4 = (f32[512,512]{0,1:T(8,128)S(1)}, f32[512,512]{0,1:T(8,128)S(1)}, u32[]{:S(2)}, u32[]{:S(2)}) collective-permute-start(f32[512,512]{0,1:T(8,128)S(1)} %slice_subtract_fusion.2), channel_id=1, source_target_pairs={{0,16},{1,17},{2,18},{3,19},{4,20},{5,21},{6,22},{7,23},{8,24},{9,... | collective-permute-start | bytes 3145736 | tf_op jit(solution)/shard_map/ppermute | solution.py:10
  116.1 20.8 %collective-permute-done.4 = f32[512,512]{0,1:T(8,128)S(1)} collective-permute-done((f32[512,512]{0,1:T(8,128)S(1)}, f32[512,512]{0,1:T(8,128)S(1)}, u32[]{:S(2)}, u32[]{:S(2)}) %collective-permute-start.4) | collective-permute-done | bytes 1048608 | tf_op jit(solution)/shard_map/ppermute | solution.py:10
  136.8 0.4 maximum_select_fusion.4
  137.2 3.0 %fusion.5 = f32[512,512]{1,0:T(8,128)S(1)} fusion(f32[1024,512]{0,1:T(8,128)S(1)} %maximum_select_fusion.4, bf16[1,1,5,1024,512]{4,3,2,1,0:T(8,128)(2,1)} %param.10), kind=kOutput, calls=%fused_computation.26 | convolution fusion | flops 3221225472 | bytes 4194304 | tf_op jit(solution)/shard_map/dot_general | solution.py:29
  140.3 2.0 fusion.33
  142.3 3.0 %slice_subtract_fusion.1 = f32[512,512]{0,1:T(8,128)} fusion(f32[1024,512]{0,1:T(8,128)S(1)} %maximum_select_fusion.4, f32[512,512]{1,0:T(8,128)S(1)} %fusion.33, bf16[1,1,5,1024,512]{4,3,2,1,0:T(8,128)(2,1)} %param.10), kind=kOutput, calls=%fused_computation.17 | convolution fusion | flops 1610874880 | bytes 3670016 | tf_op jit(solution)/shard_map/dot_general | solution.py:33
  145.4 1.9 collective-permute-start.5
  147.3 20.2 %collective-permute-done.5 = f32[512,512]{0,1:T(8,128)} collective-permute-done((f32[512,512]{0,1:T(8,128)}, f32[512,512]{0,1:T(8,128)}, u32[]{:S(2)}, u32[]{:S(2)}) %collective-permute-start.5) | collective-permute-done | bytes 1048608 | tf_op jit(solution)/shard_map/ppermute | solution.py:10
  167.5 2.6 %maximum_select_fusion.5 = f32[1024,512]{0,1:T(8,128)S(1)} fusion(f32[512,512]{0,1:T(8,128)} %collective-permute-done.5, f32[512,512]{0,1:T(8,128)} %slice_subtract_fusion.1, pred[]{:T(512)S(6)} %eq.22), kind=kLoop, calls=%fused_computation.5 | loop fusion | flops 1572864 | bytes 4194305 | tf_op jit(solution)/shard_map/jit(_where)/select_n | solution.py:41
  170.1 1.8 fusion.3
  171.9 1.0 fusion.28
  172.9 2.0 slice_subtract_fusion
  174.9 3.8 %collective-permute-start.6 = (f32[512,512]{0,1:T(8,128)}, f32[512,512]{0,1:T(8,128)}, u32[]{:S(2)}, u32[]{:S(2)}) collective-permute-start(f32[512,512]{0,1:T(8,128)} %slice_subtract_fusion), channel_id=1, source_target_pairs={{0,64},{32,96},{64,0},{96,32},{1,65},{33,97},{65,1},{97,33},{2,66}... | collective-permute-start | bytes 3145736 | tf_op jit(solution)/shard_map/ppermute | solution.py:10
  178.7 19.3 %collective-permute-done.6 = f32[512,512]{0,1:T(8,128)} collective-permute-done((f32[512,512]{0,1:T(8,128)}, f32[512,512]{0,1:T(8,128)}, u32[]{:S(2)}, u32[]{:S(2)}) %collective-permute-start.6) | collective-permute-done | bytes 1048608 | tf_op jit(solution)/shard_map/ppermute | solution.py:10
  198.0 2.6 %maximum_select_fusion.6 = f32[1024,512]{0,1:T(8,128)S(1)} fusion(f32[512,512]{0,1:T(8,128)} %collective-permute-done.6, f32[512,512]{0,1:T(8,128)} %slice_subtract_fusion, pred[]{:T(512)S(6)} %eq.21), kind=kLoop, calls=%fused_computation.6 | loop fusion | flops 1572864 | bytes 4194305 | tf_op jit(solution)/shard_map/jit(_where)/select_n | solution.py:41
  200.6 1.8 fusion.1
  202.4 1.2 copy-done.4
  203.6 1.0 fusion.23
  204.6 1.0 convolution_bitcast_fusion
  205.7 0.6 fusion.72
  (15 shorter events, 0.1 us)
Async XLA Ops:
  0.0 2.6 %copy-start = (bf16[1,512,512]{2,1,0:T(8,128)(2,1)S(1)}, bf16[1,512,512]{2,1,0:T(8,128)(2,1)}, u32[]{:S(2)}) copy-start(bf16[1,512,512]{2,1,0:T(8,128)(2,1)} %param.9) | copy-start | bytes 1572868
  0.0 2.4 %slice-start.1 = ((bf16[1024,512]{1,0:T(8,128)(2,1)}), bf16[512,512]{1,0:T(8,128)(2,1)S(1)}, s32[]{:S(2)}) async-start(bf16[1024,512]{1,0:T(8,128)(2,1)} %param.7), calls=%async_computation.1 | async-start | bytes 1048576 | tf_op jit(solution)/shard_map/slice | solution.py:21
  2.6 1.2 copy-start.5
  4.9 2.7 %collective-permute-start = (f32[512,512]{0,1:T(8,128)S(1)}, f32[512,512]{0,1:T(8,128)S(1)}, u32[]{:S(2)}, u32[]{:S(2)}) collective-permute-start(f32[512,512]{0,1:T(8,128)S(1)} %fusion), channel_id=1, source_target_pairs={{0,1},{1,0},{2,3},{3,2},{4,5},{5,4},{6,7},{7,6},{8,9},{9,8},{10,11... | collective-permute-start | bytes 3145736 | tf_op jit(solution)/shard_map/ppermute | solution.py:10
  15.1 25.3 %collective-permute-start.1 = (f32[512,512]{0,1:T(8,128)S(1)}, f32[512,512]{0,1:T(8,128)S(1)}, u32[]{:S(2)}, u32[]{:S(2)}) collective-permute-start(f32[512,512]{0,1:T(8,128)S(1)} %slice_subtract_fusion.5), channel_id=1, source_target_pairs={{0,2},{1,3},{2,0},{3,1},{4,6},{5,7},{6,4},{7,5},{8,10},{9,11},{10,... | collective-permute-start | bytes 3145736 | tf_op jit(solution)/shard_map/ppermute | solution.py:10
  48.0 26.1 %collective-permute-start.2 = (f32[512,512]{0,1:T(8,128)S(1)}, f32[512,512]{0,1:T(8,128)S(1)}, u32[]{:S(2)}, u32[]{:S(2)}) collective-permute-start(f32[512,512]{0,1:T(8,128)S(1)} %slice_subtract_fusion.4), channel_id=1, source_target_pairs={{0,4},{1,5},{2,6},{3,7},{4,0},{5,1},{6,2},{7,3},{8,12},{9,13},{10,... | collective-permute-start | bytes 3145736 | tf_op jit(solution)/shard_map/ppermute | solution.py:10
  81.7 23.5 %collective-permute-start.3 = (f32[512,512]{0,1:T(8,128)S(1)}, f32[512,512]{0,1:T(8,128)S(1)}, u32[]{:S(2)}, u32[]{:S(2)}) collective-permute-start(f32[512,512]{0,1:T(8,128)S(1)} %slice_subtract_fusion.3), channel_id=1, source_target_pairs={{0,8},{1,9},{2,10},{3,11},{4,12},{5,13},{6,14},{7,15},{8,0},{9,1},... | collective-permute-start | bytes 3145736 | tf_op jit(solution)/shard_map/ppermute | solution.py:10
  112.7 24.1 %collective-permute-start.4 = (f32[512,512]{0,1:T(8,128)S(1)}, f32[512,512]{0,1:T(8,128)S(1)}, u32[]{:S(2)}, u32[]{:S(2)}) collective-permute-start(f32[512,512]{0,1:T(8,128)S(1)} %slice_subtract_fusion.2), channel_id=1, source_target_pairs={{0,16},{1,17},{2,18},{3,19},{4,20},{5,21},{6,22},{7,23},{8,24},{9,... | collective-permute-start | bytes 3145736 | tf_op jit(solution)/shard_map/ppermute | solution.py:10
  145.4 22.1 %collective-permute-start.5 = (f32[512,512]{0,1:T(8,128)}, f32[512,512]{0,1:T(8,128)}, u32[]{:S(2)}, u32[]{:S(2)}) collective-permute-start(f32[512,512]{0,1:T(8,128)} %slice_subtract_fusion.1), channel_id=1, source_target_pairs={{0,32},{32,0},{64,96},{96,64},{1,33},{33,1},{65,97},{97,65},{2,34}... | collective-permute-start | bytes 3145736 | tf_op jit(solution)/shard_map/ppermute | solution.py:10
  147.3 22.8 %copy-start.2 = (bf16[1,1,2,1024,512]{4,3,2,1,0:T(8,128)(2,1)S(1)}, bf16[1,1,2,1024,512]{4,3,2,1,0:T(8,128)(2,1)}, u32[]{:S(2)}) copy-start(bf16[1,1,2,1024,512]{4,3,2,1,0:T(8,128)(2,1)} %param.12) | copy-start | bytes 6291460
  170.1 1.8 copy-start.3
  174.9 23.0 %collective-permute-start.6 = (f32[512,512]{0,1:T(8,128)}, f32[512,512]{0,1:T(8,128)}, u32[]{:S(2)}, u32[]{:S(2)}) collective-permute-start(f32[512,512]{0,1:T(8,128)} %slice_subtract_fusion), channel_id=1, source_target_pairs={{0,64},{32,96},{64,0},{96,32},{1,65},{33,97},{65,1},{97,33},{2,66}... | collective-permute-start | bytes 3145736 | tf_op jit(solution)/shard_map/ppermute | solution.py:10
  200.6 1.8 copy-start.1
  202.4 1.2 copy-start.4
  203.6 2.0 slice-start
where the time goes:
time: 207 us; the launch traced here: 206 us
  waiting for transfers between devices  131 us (63%)
  matrix products  49.6 us (24%)
  starting transfers between devices  15.8 us (8%)
  other arithmetic  7.77 us (4%)
    ppermute x7, waiting for transfers between devices, partner_2(): lax.ppermute(array, axis, [(i, i ^ 1 << stride) for i in range(lax.axis_s...  131 us
    dot_general x7, matrix products, node_reflect(): lax.dot_general(basis, panel_rows, contract, precision=lax.Precision.HIGH...  18.7 us
    ppermute x7, starting transfers between devices, partner_2(): lax.ppermute(array, axis, [(i, i ^ 1 << stride) for i in range(lax.axis_s...  15.8 us
    dot_general x7, matrix products, node_reflect(): jnp.dot(basis[:rank_width], mixing, precision=lax.Precision.HIGHEST)  14.3 us
    dot_general x7, matrix products, node_reflect(): lax.dot_general(triangle.astype(jnp.float32), projected, contract, precis...  12.2 us
    select_n x7, other arithmetic, pair_rows(): return jnp.where(parity == 0, lower_first, upper_first)  7.16 us
  transfers between devices with their start and end apart: 7, of which 7 were waited for; matrix products, arithmetic and copies ran while one was open for 0% of the time, Pallas kernels for 0%

commit v1 on v0

v1 whole, which is shorter than its diff:
```python
import functools

import jax
import jax.numpy as jnp
from jax import lax
from jax.experimental import pallas as pl
from jax.experimental.pallas import tpu as pltpu
from jax.sharding import Mesh, PartitionSpec as P

F32 = jnp.float32
BF16 = jnp.bfloat16
NT = (((1,), (1,)), ((), ()))
NN = (((1,), (0,)), ((), ()))
VMEM = pl.BlockSpec(memory_space=pltpu.VMEM)
ANY = pl.BlockSpec(memory_space=pl.ANY)


def split_dot(rows, weights, dims):
    count = rows.shape[0]
    high = rows.astype(BF16)
    low = (rows - high.astype(F32)).astype(BF16)
    both = lax.dot_general(
        jnp.concatenate([high, low], axis=0), weights, dims, preferred_element_type=F32
    )
    return both[:count] + both[count:]


def leaf_kernel(take_other, x_ref, v_ref, f_ref, out_ref):
    half, width = out_ref.shape
    core = lax.axis_index("core")
    side = 1 - core if take_other else core
    row = lax.broadcasted_iota(jnp.int32, (half, 2 * half), 0)
    column = lax.broadcasted_iota(jnp.int32, (half, 2 * half), 1)
    wanted = (row // 4) * 8 + side * 4 + row % 4
    pick = jnp.where(column == wanted, 1.0, 0.0).astype(BF16)
    panel = lax.dot_general(pick, x_ref[...], NT, preferred_element_type=F32)
    projected = lax.dot_general(panel.astype(BF16), v_ref[...], NN, preferred_element_type=F32)
    mixing = split_dot(projected, f_ref[...], NN)
    out_ref[...] = panel[:, :width] - split_dot(mixing, v_ref[:width, :], NT)


def chain_kernel(own_ref, other_ref, ib_ref, it_ref, ob_ref, ot_ref, out_ref, v_buf, f_buf, sems):
    width = own_ref.shape[1]
    inner = ib_ref.shape[0]
    levels = v_buf.shape[0]

    def copies(level):
        basis, tri = (ib_ref, it_ref) if level < inner else (ob_ref, ot_ref)
        at = level if level < inner else level - inner
        return (
            pltpu.make_async_copy(basis.at[at], v_buf.at[level], sems.at[level, 0]),
            pltpu.make_async_copy(tri.at[at], f_buf.at[level], sems.at[level, 1]),
        )

    for level in range(levels):
        for copy in copies(level):
            copy.start()
    core = lax.axis_index("core")
    place = lax.axis_index("group") * lax.axis_size("chip") + lax.axis_index("chip")
    for level in range(levels):
        for copy in copies(level):
            copy.wait()
        if level == 0:
            own, other = own_ref[...], other_ref[...]
            base = jnp.where(core == 0, own, other)
            joined = jnp.concatenate([base, jnp.where(core == 0, other, own)], axis=1)
            projected = split_dot(joined, v_buf[level], NN)
        else:
            bit = jnp.right_shift(place, level - 1) & 1
            base = jnp.where(bit == 0, summit, 0.0)
            start = pl.multiple_of(bit * width, width)
            projected = split_dot(summit, v_buf[level, pl.ds(start, width), :], NN)
        mixing = split_dot(projected, f_buf[level], NN)
        summit = base - split_dot(mixing, v_buf[level, :width, :], NT)
    out_ref[...] = summit


def per_device(matrix, leaf_basis, leaf_tri, inner_basis, inner_tri, outer_basis, outer_tri):
    width = leaf_tri.shape[-1]
    half = matrix.shape[1] // 2
    levels = inner_basis.shape[2] + outer_basis.shape[2]

    def leaf(take_other):
        return pl.pallas_call(
            functools.partial(leaf_kernel, take_other),
            out_shape=jax.ShapeDtypeStruct((half, width), F32),
            in_specs=[VMEM] * 3,
            out_specs=VMEM,
            cost_estimate=pl.CostEstimate(
                flops=2 * 4 * width**3, bytes_accessed=4 * 2**20, transcendentals=0
            ),
            compiler_params=pltpu.CompilerParams(vmem_limit_bytes=24 * 2**20),
        )(matrix, leaf_basis, leaf_tri[0])

    sent = leaf(True)
    other = lax.ppermute(sent, "core", [(0, 1), (1, 0)])
    own = leaf(False)
    terms = pl.pallas_call(
        chain_kernel,
        out_shape=jax.ShapeDtypeStruct((half, width), F32),
        in_specs=[VMEM, VMEM, ANY, ANY, ANY, ANY],
        out_specs=VMEM,
        scratch_shapes=[
            pltpu.VMEM((levels, 2 * width, width), BF16),
            pltpu.VMEM((levels, width, width), BF16),
            pltpu.SemaphoreType.DMA((levels, 2)),
        ],
        cost_estimate=pl.CostEstimate(
            flops=2 * 22 * width**3, bytes_accessed=12 * 2**20, transcendentals=0
        ),
        compiler_params=pltpu.CompilerParams(vmem_limit_bytes=40 * 2**20),
    )(own, other, inner_basis[0, 0], inner_tri[0, 0], outer_basis[0, 0], outer_tri[0, 0])
    chips = lax.axis_size("group") * lax.axis_size("chip")
    blocks = terms.reshape(chips, half // chips, width)
    swapped = lax.all_to_all(blocks, ("group", "chip"), 0, 0, tiled=True)
    return jnp.sum(swapped, axis=0).T.astype(BF16)


def solution(mesh):
    groups, leaves = mesh.devices.shape
    fine = Mesh(mesh.devices.reshape(groups, leaves // 2, 2), ("group", "chip", "core"))
    every = ("group", "chip", "core")
    leaf = ("chip", "core")
    placed = (
        P(every, None),
        P(every, None),
        P(every, None, None),
        P("group", leaf, None, None, None),
        P("group", leaf, None, None, None),
        P("group", leaf, None, None, None),
        P("group", leaf, None, None, None),
    )
    return jax.shard_map(
        per_device, mesh=fine, in_specs=placed, out_specs=P(None, every), check_vma=False
    )
```

time: 207 us -> 45 us (0.22)
  waiting for transfers between devices: 131 us -> 0.45 us
  matrix products: 49.6 us -> 0 us
  blocking collectives: 0 us -> 24.9 us
  starting transfers between devices: 15.8 us -> 0.09 us
  Pallas kernels: 0 us -> 11.9 us
  other arithmetic: 7.77 us -> 0.7 us
  local copies, waits for them, and re-layouts: 1.65 us -> 6.55 us
    ppermute x7 -> x1, waiting for transfers between devices: 131 us -> 0.45 us  [per_device(): other = lax.ppermute(sent, 'core', [(0, 1), (1, 0)])]
    dot_general x24 -> x0, matrix products: 49.6 us -> none  [the longest x7 18.7 us: node_reflect(): lax.dot_general(basis, panel_rows, contract, precision=lax.Precision.HIGH...]
    all_to_all x0 -> x1, blocking collectives: none -> 24.9 us  [per_device(): swapped = lax.all_to_all(blocks, ('group', 'chip'), 0, 0, tiled=True)]
    ppermute x7 -> x1, starting transfers between devices: 15.8 us -> 0.09 us  [per_device(): other = lax.ppermute(sent, 'core', [(0, 1), (1, 0)])]
    pallas_call x0 -> x3, Pallas kernels: none -> 11.9 us  [the longest x1 9.06 us: per_device(): pl.pallas_call(chain_kernel, out_shape=jax.ShapeDtypeStruct((half, width)...]
    select_n x7 -> x0, other arithmetic: 7.16 us -> none  [pair_rows(): return jnp.where(parity == 0, lower_first, upper_first)]
    unnamed x13 -> x14, local copies, waits for them, and re-layouts: 1.64 us -> 6.4 us
  transfers between devices with their start and end apart: 7 -> 1, of which waited for: 7 -> 1; matrix products, arithmetic and copies ran while one was open for 0% -> 0% of each run, Pallas kernels for 0% -> 3%
where the time goes in v1:
time: 45 us; the launch traced here: 44.7 us
  blocking collectives  24.9 us (55%)
  Pallas kernels  11.9 us (26%)
  local copies, waits for them, and re-layouts  6.55 us (15%)
  other arithmetic  0.7 us (2%)
  waiting for transfers between devices  0.45 us (1%)
    all_to_all x1, blocking collectives, per_device(): swapped = lax.all_to_all(blocks, ('group', 'chip'), 0, 0, tiled=True)  24.9 us
    pallas_call x1, Pallas kernels, per_device(): pl.pallas_call(chain_kernel, out_shape=jax.ShapeDtypeStruct((half, width)...  9.06 us
    unnamed x14, local copies, waits for them, and re-layouts  6.4 us
    pallas_call x2, Pallas kernels, leaf(): pl.pallas_call(functools.partial(leaf_kernel, take_other), out_shape=jax....  2.88 us
  transfers between devices with their start and end apart: 1, of which 1 were waited for; matrix products, arithmetic and copies ran while one was open for 0% of the time, Pallas kernels for 3%

profile of v1, /device:TPU:0, one launch (start us, length us, event | category | flops | bytes accessed | tf_op | source)
XLA Modules:
  0.0 44.7 jit_solution(16084594532179570655)
XLA Ops:
  0.0 0.0 copy-start.3
  0.0 1.2 %copy-done.3 = bf16[1024,512]{1,0:T(8,128)(2,1)S(1)} copy-done((bf16[1024,512]{1,0:T(8,128)(2,1)S(1)}, bf16[1024,512]{1,0:T(8,128)(2,1)}, u32[]{:S(2)}) %copy-start.3) | copy-done | bytes 1048600
  1.2 0.0 copy-start.4
  1.2 1.2 %copy-done.4 = bf16[1024,512]{1,0:T(8,128)(2,1)S(1)} copy-done((bf16[1024,512]{1,0:T(8,128)(2,1)S(1)}, bf16[1024,512]{1,0:T(8,128)(2,1)}, u32[]{:S(2)}) %copy-start.4) | copy-done | bytes 1048600
  2.5 0.0 copy-start.6
  2.5 1.0 %copy-done.6 = bf16[1,512,512]{2,1,0:T(8,128)(2,1)S(1)} copy-done((bf16[1,512,512]{2,1,0:T(8,128)(2,1)S(1)}, bf16[1,512,512]{2,1,0:T(8,128)(2,1)}, u32[]{:S(2)}) %copy-start.6) | copy-done | bytes 524312
  3.5 0.0 copy-start
  3.5 1.4 %shard_map.74 = f32[256,512]{1,0:T(8,128)S(1)} custom-call(bf16[1024,512]{1,0:T(8,128)(2,1)S(1)} %copy-done.3, bf16[1024,512]{1,0:T(8,128)(2,1)S(1)} %copy-done.4, bf16[512,512]{1,0:T(8,128)(2,1)S(1)} %bitcast.12), custom_call_target="tpu_custom_call" | custom-call | flops 1073741824 | bytes 4194304 | tf_op jit(solution)/shard_map/pallas_call | solution.py:84
  4.9 0.0 copy-start.1
  5.0 0.1 collective-permute-start
  5.0 1.4 %shard_map.73.own_ref = f32[256,512]{1,0:T(8,128)S(1)} custom-call(bf16[1024,512]{1,0:T(8,128)(2,1)S(1)} %copy-done.3, bf16[1024,512]{1,0:T(8,128)(2,1)S(1)} %copy-done.4, bf16[512,512]{1,0:T(8,128)(2,1)S(1)} %bitcast.13), custom_call_target="tpu_custom_call" | custom-call | flops 1073741824 | bytes 4194304 | tf_op jit(solution)/shard_map/pallas_call | solution.py:84
  6.5 0.5 %collective-permute-done.other_ref = f32[256,512]{1,0:T(8,128)S(1)} collective-permute-done((f32[256,512]{1,0:T(8,128)S(1)}, f32[256,512]{1,0:T(8,128)S(1)}, u32[]{:S(2)}, u32[]{:S(2)}) %collective-permute-start) | collective-permute-done | bytes 524320 | tf_op jit(solution)/shard_map/ppermute | solution.py:96
  6.9 0.0 copy-done
  6.9 0.1 copy-done.1
  7.0 0.0 copy-start.2
  7.0 1.6 %copy-done.2 = bf16[1,1,2,1024,512]{4,3,2,1,0:T(8,128)(2,1)S(1)} copy-done((bf16[1,1,2,1024,512]{4,3,2,1,0:T(8,128)(2,1)S(1)}, bf16[1,1,2,1024,512]{4,3,2,1,0:T(8,128)(2,1)}, u32[]{:S(2)}) %copy-start.2) | copy-done | bytes 2097176
  8.6 0.0 copy-start.5
  8.6 1.2 %copy-done.5 = bf16[1,1,2,512,512]{4,3,2,1,0:T(8,128)(2,1)S(1)} copy-done((bf16[1,1,2,512,512]{4,3,2,1,0:T(8,128)(2,1)S(1)}, bf16[1,1,2,512,512]{4,3,2,1,0:T(8,128)(2,1)}, u32[]{:S(2)}) %copy-start.5) | copy-done | bytes 1048600
  9.9 9.1 %shard_map.75 = f32[256,512]{1,0:T(8,128)S(1)} custom-call(f32[256,512]{1,0:T(8,128)S(1)} %shard_map.73.own_ref, f32[256,512]{1,0:T(8,128)S(1)} %collective-permute-done.other_ref, bf16[5,1024,512]{2,1,0:T(8,128)(2,1)S(1)} %bitcast.8, bf16[5,512,512]{2,1,0:T(8,128)(2,1)S(1)} %bitcast.9, bf16[2,1024,512]{2,1,0:T(8,128)(2,1)S(1)} %bitcast.10, ...), custom_call_target="tpu_custom_call" | custom-call | flops 5905580032 | bytes 12582912 | tf_op jit(solution)/shard_map/pallas_call | solution.py:98
  18.9 0.1 reshape.3
  19.1 24.9 %all_to_all.5 = f32[64,4,512]{2,1,0:T(4,128)S(1)} all-to-all(f32[64,4,512]{2,1,0:T(4,128)S(1)} %reshape.3), channel_id=1, replica_groups=mesh['group'=4,'chip'=16,'core'=2] {'group','chip'}, dimensions={0} | all-to-all | bytes 1048576 | tf_op jit(solution)/shard_map/all_to_all | solution.py:115
  44.0 0.7 %reduce_sum.9 = bf16[4,512]{1,0:T(4,128)(2,1)} reduce(f32[64,4,512]{2,1,0:T(4,128)S(1)} %all_to_all.5, f32[]{:T(128)} %constant.0.clone.1), dimensions={0}, to_apply=%region_0.0 | reduce | flops 129024 | bytes 528388 | tf_op jit(solution)/shard_map/reduce_sum | solution.py:116
Async XLA Ops:
  0.0 1.2 %copy-start.3 = (bf16[1024,512]{1,0:T(8,128)(2,1)S(1)}, bf16[1024,512]{1,0:T(8,128)(2,1)}, u32[]{:S(2)}) copy-start(bf16[1024,512]{1,0:T(8,128)(2,1)} %x_ref.3) | copy-start | bytes 3145732
  1.2 1.2 %copy-start.4 = (bf16[1024,512]{1,0:T(8,128)(2,1)S(1)}, bf16[1024,512]{1,0:T(8,128)(2,1)}, u32[]{:S(2)}) copy-start(bf16[1024,512]{1,0:T(8,128)(2,1)} %v_ref.3) | copy-start | bytes 3145732
  2.5 1.0 %copy-start.6 = (bf16[1,512,512]{2,1,0:T(8,128)(2,1)S(1)}, bf16[1,512,512]{2,1,0:T(8,128)(2,1)}, u32[]{:S(2)}) copy-start(bf16[1,512,512]{2,1,0:T(8,128)(2,1)} %param.9) | copy-start | bytes 1572868
  3.5 3.5 %copy-start = (bf16[1,1,5,1024,512]{4,3,2,1,0:T(8,128)(2,1)S(1)}, bf16[1,1,5,1024,512]{4,3,2,1,0:T(8,128)(2,1)}, u32[]{:S(2)}) copy-start(bf16[1,1,5,1024,512]{4,3,2,1,0:T(8,128)(2,1)} %param.10) | copy-start | bytes 15728644
  4.9 2.1 %copy-start.1 = (bf16[1,1,5,512,512]{4,3,2,1,0:T(8,128)(2,1)S(1)}, bf16[1,1,5,512,512]{4,3,2,1,0:T(8,128)(2,1)}, u32[]{:S(2)}) copy-start(bf16[1,1,5,512,512]{4,3,2,1,0:T(8,128)(2,1)} %param.11) | copy-start | bytes 7864324
  5.0 2.0 %collective-permute-start = (f32[256,512]{1,0:T(8,128)S(1)}, f32[256,512]{1,0:T(8,128)S(1)}, u32[]{:S(2)}, u32[]{:S(2)}) collective-permute-start(f32[256,512]{1,0:T(8,128)S(1)} %shard_map.74), channel_id=1, source_target_pairs={{0,1},{1,0},{2,3},{3,2},{4,5},{5,4},{6,7},{7,6},{8,9},{9,8},{10,11... | collective-permute-start | bytes 1572872 | tf_op jit(solution)/shard_map/ppermute | solution.py:96
  7.0 1.6 %copy-start.2 = (bf16[1,1,2,1024,512]{4,3,2,1,0:T(8,128)(2,1)S(1)}, bf16[1,1,2,1024,512]{4,3,2,1,0:T(8,128)(2,1)}, u32[]{:S(2)}) copy-start(bf16[1,1,2,1024,512]{4,3,2,1,0:T(8,128)(2,1)} %param.12) | copy-start | bytes 6291460
  8.6 1.2 %copy-start.5 = (bf16[1,1,2,512,512]{4,3,2,1,0:T(8,128)(2,1)S(1)}, bf16[1,1,2,512,512]{4,3,2,1,0:T(8,128)(2,1)}, u32[]{:S(2)}) copy-start(bf16[1,1,2,512,512]{4,3,2,1,0:T(8,128)(2,1)} %param.13) | copy-start | bytes 3145732

commit v2 on v1

v2 whole, which is shorter than its diff:
```python
import functools

import jax
import jax.numpy as jnp
from jax import lax
from jax.experimental import pallas as pl
from jax.experimental.pallas import tpu as pltpu
from jax.sharding import Mesh, PartitionSpec as P

PIECES = 1
F32 = jnp.float32
BF16 = jnp.bfloat16
NT = (((1,), (1,)), ((), ()))
NN = (((1,), (0,)), ((), ()))
VMEM = pl.BlockSpec(memory_space=pltpu.VMEM)
HBM = pl.BlockSpec(memory_space=pltpu.HBM)


def split_dot(rows, weights, dims):
    count = rows.shape[0]
    high = rows.astype(BF16)
    low = (rows - high.astype(F32)).astype(BF16)
    both = lax.dot_general(
        jnp.concatenate([high, low], axis=0), weights, dims, preferred_element_type=F32
    )
    return both[:count] + both[count:]


def pick_rows(side, half):
    row = lax.broadcasted_iota(jnp.int32, (half, 2 * half), 0)
    column = lax.broadcasted_iota(jnp.int32, (half, 2 * half), 1)
    wanted = (row // 4) * 8 + side * 4 + row % 4
    return jnp.where(column == wanted, 1.0, 0.0).astype(BF16)


def mix_dot(rows, triangle):
    half = triangle.shape[0] // 2
    left = split_dot(rows[:, :half], triangle[:half, :half], NN)
    right = split_dot(rows, triangle[:, half:], NN)
    return jnp.concatenate([left, right], axis=1)


def fetch(sources, targets, sems):
    copies = [
        pltpu.make_async_copy(source, target, sems.at[index])
        for index, (source, target) in enumerate(zip(sources, targets, strict=True))
    ]
    for copy in copies:
        copy.start()
    return copies


def finish_leaf(top, projected, v_ref, f_ref):
    mixing = mix_dot(projected, f_ref[...])
    return top - split_dot(mixing, v_ref[: f_ref.shape[0], :], NT)


def send_kernel(x_hbm, v_hbm, f_hbm, ib_hbm, it_hbm, out_ref, x_ref, v_ref, f_ref, wv_ref, wf_ref, sems):
    rows = x_hbm.shape[0]
    size = rows // PIECES
    spans = [pl.ds(piece * size, size) for piece in range(PIECES)]
    sources = [ref.at[span] for ref in (x_hbm, v_hbm) for span in spans]
    targets = [ref.at[span] for ref in (x_ref, v_ref) for span in spans]
    sources.append(f_hbm)
    targets.append(f_ref)
    for level in range(wv_ref.shape[0]):
        sources += [ib_hbm.at[level], it_hbm.at[level]]
        targets += [wv_ref.at[level], wf_ref.at[level]]
    copies = fetch(sources, targets, sems)
    pick = pick_rows(1 - lax.axis_index("core"), out_ref.shape[0])
    for copy in copies[:PIECES]:
        copy.wait()
    panel = lax.dot_general(pick, x_ref[...], NT, preferred_element_type=F32)
    for copy in copies[PIECES : 2 * PIECES + 1]:
        copy.wait()
    projected = lax.dot_general(panel.astype(BF16), v_ref[...], NN, preferred_element_type=F32)
    out_ref[...] = finish_leaf(panel[:, : f_ref.shape[0]], projected, v_ref, f_ref)
    for copy in copies[2 * PIECES + 1 :]:
        copy.wait()


def keep_kernel(x_ref, v_ref, f_ref, out_ref):
    pick = pick_rows(lax.axis_index("core"), out_ref.shape[0])
    panel = lax.dot_general(pick, x_ref[...], NT, preferred_element_type=F32)
    projected = lax.dot_general(panel.astype(BF16), v_ref[...], NN, preferred_element_type=F32)
    out_ref[...] = finish_leaf(panel[:, : f_ref.shape[0]], projected, v_ref, f_ref)


def chain_kernel(
    own_ref, other_ref, wv_ref, wf_ref, ib_hbm, it_hbm, ob_hbm, ot_hbm, out_ref, v_buf, f_buf, sems
):
    width = own_ref.shape[1]
    early, inner, outer = wv_ref.shape[0], ib_hbm.shape[0], ob_hbm.shape[0]
    sources = []
    for level in range(early, inner):
        sources += [ib_hbm.at[level], it_hbm.at[level]]
    for level in range(outer):
        sources += [ob_hbm.at[level], ot_hbm.at[level]]
    late = inner + outer - early
    targets = [buf.at[index] for index in range(late) for buf in (v_buf, f_buf)]
    copies = fetch(sources, targets, sems)
    levels = [(wv_ref, wf_ref, at, []) for at in range(early)]
    levels += [(v_buf, f_buf, at, copies[2 * at : 2 * at + 2]) for at in range(late)]
    core = lax.axis_index("core")
    place = lax.axis_index("group") * lax.axis_size("chip") + lax.axis_index("chip")
    for level, (basis, tri, at, waits) in enumerate(levels):
        for copy in waits:
            copy.wait()
        if level == 0:
            own, other = own_ref[...], other_ref[...]
            base = jnp.where(core == 0, own, other)
            joined = jnp.concatenate([base, jnp.where(core == 0, other, own)], axis=1)
            projected = split_dot(joined, basis[at], NN)
        else:
            bit = jnp.right_shift(place, level - 1) & 1
            base = jnp.where(bit == 0, summit, 0.0)
            start = pl.multiple_of(bit * width, width)
            projected = split_dot(summit, basis[at, pl.ds(start, width), :], NN)
        mixing = mix_dot(projected, tri[at])
        summit = base - split_dot(mixing, basis[at, :width, :], NT)
    out_ref[...] = summit


def in_hbm(array):
    return pltpu.with_memory_space_constraint(array, pltpu.HBM)


def estimate(units, mebibytes):
    return pl.CostEstimate(
        flops=units * 2 * 512**3, bytes_accessed=mebibytes * 2**20, transcendentals=0
    )


def per_device(matrix, leaf_basis, leaf_tri, inner_basis, inner_tri, outer_basis, outer_tri):
    rows, width = leaf_basis.shape
    half = matrix.shape[1] // 2
    inner, outer = inner_basis.shape[2], outer_basis.shape[2]
    ahead = 2
    trees = (in_hbm(inner_basis[0, 0]), in_hbm(inner_tri[0, 0]))

    def basis_of(levels):
        return jax.ShapeDtypeStruct((levels, rows, width), BF16)

    def tri_of(levels):
        return jax.ShapeDtypeStruct((levels, width, width), BF16)

    summit = jax.ShapeDtypeStruct((half, width), F32)
    sent, x, v, f, wv, wf = pl.pallas_call(
        send_kernel,
        out_shape=(
            summit,
            jax.ShapeDtypeStruct(matrix.shape, BF16),
            jax.ShapeDtypeStruct((rows, width), BF16),
            jax.ShapeDtypeStruct((width, width), BF16),
            basis_of(ahead),
            tri_of(ahead),
        ),
        in_specs=[HBM] * 5,
        out_specs=(VMEM,) * 6,
        scratch_shapes=[pltpu.SemaphoreType.DMA((2 * PIECES + 1 + 2 * ahead,))],
        cost_estimate=estimate(4, 4),
        compiler_params=pltpu.CompilerParams(vmem_limit_bytes=16 * 2**20),
    )(in_hbm(matrix), in_hbm(leaf_basis), in_hbm(leaf_tri[0]), *trees)
    other = lax.ppermute(sent, "core", [(0, 1), (1, 0)])
    own = pl.pallas_call(
        keep_kernel,
        out_shape=summit,
        in_specs=[VMEM] * 3,
        out_specs=VMEM,
        cost_estimate=estimate(4, 4),
        compiler_params=pltpu.CompilerParams(vmem_limit_bytes=16 * 2**20),
    )(x, v, f)
    late = inner + outer - ahead
    terms = pl.pallas_call(
        chain_kernel,
        out_shape=summit,
        in_specs=[VMEM] * 4 + [HBM] * 4,
        out_specs=VMEM,
        scratch_shapes=[
            pltpu.VMEM((late, rows, width), BF16),
            pltpu.VMEM((late, width, width), BF16),
            pltpu.SemaphoreType.DMA((2 * late,)),
        ],
        cost_estimate=estimate(22, 12),
        compiler_params=pltpu.CompilerParams(vmem_limit_bytes=24 * 2**20),
    )(own, other, wv, wf, *trees, in_hbm(outer_basis[0, 0]), in_hbm(outer_tri[0, 0]))
    chips = lax.axis_size("group") * lax.axis_size("chip")
    blocks = terms.reshape(chips, half // chips, width)
    swapped = lax.all_to_all(blocks, ("group", "chip"), 0, 0, tiled=True)
    return jnp.sum(swapped, axis=0).T.astype(BF16)


def solution(mesh):
    groups, leaves = mesh.devices.shape
    fine = Mesh(mesh.devices.reshape(groups, leaves // 2, 2), ("group", "chip", "core"))
    every = ("group", "chip", "core")
    leaf = ("chip", "core")
    placed = (
        P(every, None),
        P(every, None),
        P(every, None, None),
        P("group", leaf, None, None, None),
        P("group", leaf, None, None, None),
        P("group", leaf, None, None, None),
        P("group", leaf, None, None, None),
    )
    return jax.shard_map(
        per_device, mesh=fine, in_specs=placed, out_specs=P(None, every), check_vma=False
    )
```

time: 45 us -> 39.2 us (0.87)
  local copies, waits for them, and re-layouts: 6.55 us -> 0.15 us
  Pallas kernels: 11.9 us -> 12.7 us
    unnamed x14 -> x0, local copies, waits for them, and re-layouts: 6.4 us -> none
    pallas_call x3, Pallas kernels: 11.9 us -> 12.7 us  [the longest x1 8.31 us: per_device(): pl.pallas_call(chain_kernel, out_shape=summit, in_specs=[VMEM] * 4 + [HBM...]
  transfers between devices with their start and end apart: 1 -> 1, of which waited for: 1 -> 1; matrix products, arithmetic and copies ran while one was open for 0% -> 0% of each run, Pallas kernels for 3% -> 4%
where the time goes in v2:
time: 39.2 us; the launch traced here: 39 us
  blocking collectives  25 us (64%)
  Pallas kernels  12.7 us (32%)
  other arithmetic  0.7 us (2%)
  waiting for transfers between devices  0.44 us (1%)
    all_to_all x1, blocking collectives, per_device(): swapped = lax.all_to_all(blocks, ('group', 'chip'), 0, 0, tiled=True)  25 us
    pallas_call x1, Pallas kernels, per_device(): pl.pallas_call(chain_kernel, out_shape=summit, in_specs=[VMEM] * 4 + [HBM...  8.31 us
    pallas_call x1, Pallas kernels, per_device(): pl.pallas_call(send_kernel, out_shape=(summit, jax.ShapeDtypeStruct(matri...  2.9 us
    pallas_call x1, Pallas kernels, per_device(): pl.pallas_call(keep_kernel, out_shape=summit, in_specs=[VMEM] * 3, out_sp...  1.45 us
  transfers between devices with their start and end apart: 1, of which 1 were waited for; matrix products, arithmetic and copies ran while one was open for 0% of the time, Pallas kernels for 4%

profile of v2, /device:TPU:0, one launch (start us, length us, event | category | flops | bytes accessed | tf_op | source)
XLA Modules:
  0.0 39.0 jit_solution(14641014367810259908)
XLA Ops:
  0.0 2.9 %shard_map.73 = (f32[256,512]{1,0:T(8,128)S(1)}, bf16[1024,512]{1,0:T(8,128)(2,1)S(1)}, bf16[1024,512]{1,0:T(8,128)(2,1)S(1)}, bf16[512,512]{1,0:T(8,128)(2,1)S(...) custom-call(bf16[1024,512]{1,0:T(8,128)(2,1)} %x_hbm.1, bf16[1024,512]{1,0:T(8,128)(2,1)} %v_hbm.1, ...), custom_call_target="tpu_custom_call" | custom-call | flops 1073741824 | bytes 4194304 | tf_op jit(solution)/shard_map/pallas_call | solution.py:148
  2.9 0.1 collective-permute-start
  3.0 1.4 %shard_map.74.own_ref = f32[256,512]{1,0:T(8,128)S(1)} custom-call(bf16[1024,512]{1,0:T(8,128)(2,1)S(1)} %get-tuple-element.11.x_ref, bf16[1024,512]{1,0:T(8,128)(2,1)S(1)} %get-tuple-element.12.v_ref, bf16[512,512]{1,0:T(8,128)(2,1)S(1)} %get-tuple-element.13.f_ref), custom_call_target="tpu_custom_call" | custom-call | flops 1073741824 | bytes 4194304 | tf_op jit(solution)/shard_map/pallas_call | solution.py:165
  4.5 0.4 %collective-permute-done.other_ref = f32[256,512]{1,0:T(8,128)S(1)} collective-permute-done((f32[256,512]{1,0:T(8,128)S(1)}, f32[256,512]{1,0:T(8,128)S(1)}, u32[]{:S(2)}, u32[]{:S(2)}) %collective-permute-start) | collective-permute-done | bytes 524320 | tf_op jit(solution)/shard_map/ppermute | solution.py:164
  4.9 8.3 %shard_map.75 = f32[256,512]{1,0:T(8,128)S(1)} custom-call(f32[256,512]{1,0:T(8,128)S(1)} %shard_map.74.own_ref, f32[256,512]{1,0:T(8,128)S(1)} %collective-permute-done.other_ref, bf16[2,1024,512]{2,1,0:T(8,128)(2,1)S(1)} %get-tuple-element.15.wv_ref, bf16[2,512,512]{2,1,0:T(8,128)(2,1)S(1)} %get-tuple-element.16.wf_ref, bf16[5,1024,512]{2,1,0:T(8,128)(2,1)} %bitcast.9, ...), custom_call_target="tpu_custom_call" | custom-call | flops 5905580032 | bytes 12582912 | tf_op jit(solution)/shard_map/pallas_call | solution.py:174
  13.2 0.1 reshape.3
  13.4 25.0 %all_to_all.5 = f32[64,4,512]{2,1,0:T(4,128)S(1)} all-to-all(f32[64,4,512]{2,1,0:T(4,128)S(1)} %reshape.3), channel_id=1, replica_groups=mesh['group'=4,'chip'=16,'core'=2] {'group','chip'}, dimensions={0} | all-to-all | bytes 1048576 | tf_op jit(solution)/shard_map/all_to_all | solution.py:189
  38.3 0.7 %reduce_sum.9 = bf16[4,512]{1,0:T(4,128)(2,1)} reduce(f32[64,4,512]{2,1,0:T(4,128)S(1)} %all_to_all.5, f32[]{:T(128)} %constant.0.clone.1), dimensions={0}, to_apply=%region_0.0 | reduce | flops 129024 | bytes 528388 | tf_op jit(solution)/shard_map/reduce_sum | solution.py:190
Async XLA Ops:
  2.9 2.0 %collective-permute-start = (f32[256,512]{1,0:T(8,128)S(1)}, f32[256,512]{1,0:T(8,128)S(1)}, u32[]{:S(2)}, u32[]{:S(2)}) collective-permute-start(f32[256,512]{1,0:T(8,128)S(1)} %get-tuple-element.14), channel_id=1, source_target_pairs={{0,1},{1,0},{2,3},{3,2},{4,5},{5,4},{6,7},{7,6},{8,9},{9,8},{10,11... | collective-permute-start | bytes 1572872 | tf_op jit(solution)/shard_map/ppermute | solution.py:164

commit v3 on v2

--- a/solution.py
+++ b/solution.py
@@ -7,23 +7,20 @@
 from jax.experimental.pallas import tpu as pltpu
 from jax.sharding import Mesh, PartitionSpec as P
 
-PIECES = 1
+NT = (((1,), (1,)), ((), ()))
+NN = (((1,), (0,)), ((), ()))
+TILE = 256
+UNITS = 2
+GROUPS = 4
 F32 = jnp.float32
 BF16 = jnp.bfloat16
-NT = (((1,), (1,)), ((), ()))
-NN = (((1,), (0,)), ((), ()))
 VMEM = pl.BlockSpec(memory_space=pltpu.VMEM)
 HBM = pl.BlockSpec(memory_space=pltpu.HBM)
 
 
-def split_dot(rows, weights, dims):
-    count = rows.shape[0]
+def pair(rows):
     high = rows.astype(BF16)
-    low = (rows - high.astype(F32)).astype(BF16)
-    both = lax.dot_general(
-        jnp.concatenate([high, low], axis=0), weights, dims, preferred_element_type=F32
-    )
-    return both[:count] + both[count:]
+    return high, (rows - high.astype(F32)).astype(BF16)
 
 
 def pick_rows(side, half):
@@ -33,11 +30,107 @@
     return jnp.where(column == wanted, 1.0, 0.0).astype(BF16)
 
 
-def mix_dot(rows, triangle):
-    half = triangle.shape[0] // 2
-    left = split_dot(rows[:, :half], triangle[:half, :half], NN)
-    right = split_dot(rows, triangle[:, half:], NN)
-    return jnp.concatenate([left, right], axis=1)
+def tile(index):
+    return slice(index * TILE, (index + 1) * TILE)
+
+
+def by_columns(depth):
+    return lambda unit: range(depth)
+
+
+def triangle_plan(unit):
+    return range(unit + 1)
+
+
+def run_stages(stages, lhs, sums):
+    groups = len(lhs)
+    slots = []
+    for index, (plan, _, _) in enumerate(stages):
+        rounds = max(len(plan(unit)) for unit in range(UNITS))
+        slots += [(index, group, at) for group in range(groups) for at in range(rounds)]
+
+    def depth_of(unit, slot):
+        index, group, at = slot
+        order = list(stages[index][0](unit))
+        order = order[::-1] if group % 2 else order
+        return order[at] if at < len(order) else None
+
+    loads = [[] for _ in range(UNITS)]
+    load_at = [{} for _ in range(UNITS)]
+    for unit in range(UNITS):
+        held = None
+        for position, slot in enumerate(slots):
+            depth = depth_of(unit, slot)
+            if depth is not None and (slot[0], depth) != held:
+                held = (slot[0], depth)
+                load_at[unit][position] = len(loads[unit])
+                loads[unit].append(held)
+    pushed = [0] * UNITS
+
+    def push(unit, count):
+        while pushed[unit] < min(count, len(loads[unit])):
+            index, depth = loads[unit][pushed[unit]]
+            matrix, transpose = stages[index][1](unit, depth)
+            pltpu.matmul_push_rhs(matrix, pushed[unit] % 2, unit, transpose=transpose)
+            pushed[unit] += 1
+
+    rows = {(0, group): lhs[group] for group in range(groups)}
+    waiting = [(index, group) for index in range(len(stages)) for group in range(groups)]
+
+    def finish():
+        index, group = waiting.pop(0)
+        tiles = [pltpu.matmul_pop(sums[unit][group]) for unit in range(UNITS)]
+        rows[index + 1, group] = stages[index][2](group, tiles)
+
+    for position, slot in enumerate(slots):
+        while slot[:2] not in rows:
+            finish()
+        for part in range(len(rows[slot[:2]][0])):
+            for unit in range(UNITS):
+                depth = depth_of(unit, slot)
+                if depth is None:
+                    continue
+                load = load_at[unit].get(position) if part == 0 else None
+                if load is not None:
+                    push(unit, load + 1)
+                pltpu.matmul_acc_lhs(
+                    sums[unit][slot[1]],
+                    rows[slot[:2]][depth][part],
+                    load_staged_rhs=None if load is None else load % 2,
+                )
+                if load is not None:
+                    push(unit, load + 2)
+    while waiting:
+        finish()
+
+
+def with_sums(body, rows):
+    def scoped(*flat):
+        body([flat[unit * GROUPS : (unit + 1) * GROUPS] for unit in range(UNITS)])
+
+    pl.run_scoped(
+        scoped,
+        *[
+            pltpu.ACC(unit)((rows // GROUPS, TILE), F32)
+            for unit in range(UNITS)
+            for _ in range(GROUPS)
+        ],
+    )
+
+
+def pairs(group, tiles):
+    return [pair(values) for values in tiles]
+
+
+def once(copies):
+    done = set()
+
+    def ready(index=0):
+        if index not in done:
+            done.add(index)
+            copies[index].wait()
+
+    return ready
 
 
 def fetch(sources, targets, sems):
@@ -50,32 +143,42 @@
     return copies
 
 
+def split_dot(rows, weights, dims):
+    count = rows.shape[0]
+    high = rows.astype(BF16)
+    low = (rows - high.astype(F32)).astype(BF16)
+    both = lax.dot_general(
+        jnp.concatenate([high, low], axis=0), weights, dims, preferred_element_type=F32
+    )
+    return both[:count] + both[count:]
+
+
+def mix_dot(rows, triangle):
+    half = triangle.shape[0] // 2
+    left = split_dot(rows[:, :half], triangle[:half, :half], NN)
+    right = split_dot(rows, triangle[:, half:], NN)
+    return jnp.concatenate([left, right], axis=1)
+
+
 def finish_leaf(top, projected, v_ref, f_ref):
     mixing = mix_dot(projected, f_ref[...])
     return top - split_dot(mixing, v_ref[: f_ref.shape[0], :], NT)
 
 
 def send_kernel(x_hbm, v_hbm, f_hbm, ib_hbm, it_hbm, out_ref, x_ref, v_ref, f_ref, wv_ref, wf_ref, sems):
-    rows = x_hbm.shape[0]
-    size = rows // PIECES
-    spans = [pl.ds(piece * size, size) for piece in range(PIECES)]
-    sources = [ref.at[span] for ref in (x_hbm, v_hbm) for span in spans]
-    targets = [ref.at[span] for ref in (x_ref, v_ref) for span in spans]
-    sources.append(f_hbm)
-    targets.append(f_ref)
+    sources, targets = [x_hbm, v_hbm, f_hbm], [x_ref, v_ref, f_ref]
     for level in range(wv_ref.shape[0]):
         sources += [ib_hbm.at[level], it_hbm.at[level]]
         targets += [wv_ref.at[level], wf_ref.at[level]]
     copies = fetch(sources, targets, sems)
     pick = pick_rows(1 - lax.axis_index("core"), out_ref.shape[0])
-    for copy in copies[:PIECES]:
-        copy.wait()
+    copies[0].wait()
     panel = lax.dot_general(pick, x_ref[...], NT, preferred_element_type=F32)
-    for copy in copies[PIECES : 2 * PIECES + 1]:
-        copy.wait()
+    copies[1].wait()
+    copies[2].wait()
     projected = lax.dot_general(panel.astype(BF16), v_ref[...], NN, preferred_element_type=F32)
     out_ref[...] = finish_leaf(panel[:, : f_ref.shape[0]], projected, v_ref, f_ref)
-    for copy in copies[2 * PIECES + 1 :]:
+    for copy in copies[3:]:
         copy.wait()
 
 
@@ -89,7 +192,8 @@
 def chain_kernel(
     own_ref, other_ref, wv_ref, wf_ref, ib_hbm, it_hbm, ob_hbm, ot_hbm, out_ref, v_buf, f_buf, sems
 ):
-    width = own_ref.shape[1]
+    rows, width = own_ref.shape
+    count = rows // GROUPS
     early, inner, outer = wv_ref.shape[0], ib_hbm.shape[0], ob_hbm.shape[0]
     sources = []
     for level in range(early, inner):
@@ -98,31 +202,75 @@
         sources += [ob_hbm.at[level], ot_hbm.at[level]]
     late = inner + outer - early
     targets = [buf.at[index] for index in range(late) for buf in (v_buf, f_buf)]
-    copies = fetch(sources, targets, sems)
-    levels = [(wv_ref, wf_ref, at, []) for at in range(early)]
-    levels += [(v_buf, f_buf, at, copies[2 * at : 2 * at + 2]) for at in range(late)]
+    arrived = once(fetch(sources, targets, sems))
     core = lax.axis_index("core")
     place = lax.axis_index("group") * lax.axis_size("chip") + lax.axis_index("chip")
-    for level, (basis, tri, at, waits) in enumerate(levels):
-        for copy in waits:
-            copy.wait()
-        if level == 0:
-            own, other = own_ref[...], other_ref[...]
-            base = jnp.where(core == 0, own, other)
-            joined = jnp.concatenate([base, jnp.where(core == 0, other, own)], axis=1)
-            projected = split_dot(joined, basis[at], NN)
-        else:
-            bit = jnp.right_shift(place, level - 1) & 1
-            base = jnp.where(bit == 0, summit, 0.0)
-            start = pl.multiple_of(bit * width, width)
-            projected = split_dot(summit, basis[at, pl.ds(start, width), :], NN)
-        mixing = mix_dot(projected, tri[at])
-        summit = base - split_dot(mixing, basis[at, :width, :], NT)
-    out_ref[...] = summit
+    summit = [None] * GROUPS
+
+    def level_stages(level):
+        basis_ref, tri_ref, at = (
+            (wv_ref, wf_ref, level) if level < early else (v_buf, f_buf, level - early)
+        )
+        bit = jnp.right_shift(place, level - 1) & 1 if level else 0
+        first = bit * width
+
+        def basis(out, depth):
+            if level >= early:
+                arrived(2 * at)
+            start = pl.multiple_of(first + depth * TILE, TILE)
+            return basis_ref[at, pl.ds(start, TILE), tile(out)], False
+
+        def triangle(out, depth):
+            if level >= early:
+                arrived(2 * at + 1)
+            return tri_ref[at, tile(depth), tile(out)], False
+
+        def top(out, depth):
+            return basis_ref[at, tile(out), tile(depth)], True
+
+        def after(group, tiles):
+            base = summit[group]
+            if level:
+                base = [jnp.where(bit == 0, values, 0.0) for values in base]
+            summit[group] = [kept - values for kept, values in zip(base, tiles, strict=True)]
+            return pairs(group, summit[group])
+
+        def last(group, tiles):
+            after(group, tiles)
+            left, right = summit[group]
+            upper = lax.broadcasted_iota(jnp.int32, (count, TILE), 0) % 8 < 4
+            even = jnp.where(upper, left, pltpu.roll(right, 4, 0))
+            odd = jnp.where(upper, pltpu.roll(left, count - 4, 0), right)
+            for index, values in enumerate((even, odd)):
+                at = pl.ds(group * count // 8, count // 8)
+                out_ref[at, index] = values.reshape(count // 8, 8, TILE)
+
+        end = last if level == inner + outer - 1 else after
+        return [
+            (by_columns(2 if level else 4), basis, pairs),
+            (triangle_plan, triangle, pairs),
+            (by_columns(2), top, end),
+        ]
+
+    lhs = []
+    for group in range(GROUPS):
+        at = pl.ds(group * count, count)
+        own = [own_ref[at, tile(out)] for out in range(2)]
+        other = [other_ref[at, tile(out)] for out in range(2)]
+        summit[group] = [jnp.where(core == 0, a, b) for a, b in zip(own, other, strict=True)]
+        upper = [jnp.where(core == 0, b, a) for a, b in zip(own, other, strict=True)]
+        lhs.append(pairs(group, summit[group] + upper))
+    stages = [stage for level in range(inner + outer) for stage in level_stages(level)]
+    with_sums(lambda sums: run_stages(stages, lhs, sums), rows)
 
 
 def in_hbm(array):
     return pltpu.with_memory_space_constraint(array, pltpu.HBM)
+
+
+def sum_kernel(terms_ref, out_ref):
+    total = jnp.sum(terms_ref[...], axis=0)
+    out_ref[...] = jnp.concatenate([total[:4], total[4:]], axis=1).astype(BF16)
 
 
 def estimate(units, mebibytes):
@@ -157,7 +305,7 @@
         ),
         in_specs=[HBM] * 5,
         out_specs=(VMEM,) * 6,
-        scratch_shapes=[pltpu.SemaphoreType.DMA((2 * PIECES + 1 + 2 * ahead,))],
+        scratch_shapes=[pltpu.SemaphoreType.DMA((3 + 2 * ahead,))],
         cost_estimate=estimate(4, 4),
         compiler_params=pltpu.CompilerParams(vmem_limit_bytes=16 * 2**20),
     )(in_hbm(matrix), in_hbm(leaf_basis), in_hbm(leaf_tri[0]), *trees)
@@ -173,7 +321,7 @@
     late = inner + outer - ahead
     terms = pl.pallas_call(
         chain_kernel,
-        out_shape=summit,
+        out_shape=jax.ShapeDtypeStruct((half // 8, 2, 8, TILE), F32),
         in_specs=[VMEM] * 4 + [HBM] * 4,
         out_specs=VMEM,
         scratch_shapes=[
@@ -185,9 +333,16 @@
         compiler_params=pltpu.CompilerParams(vmem_limit_bytes=24 * 2**20),
     )(own, other, wv, wf, *trees, in_hbm(outer_basis[0, 0]), in_hbm(outer_tri[0, 0]))
     chips = lax.axis_size("group") * lax.axis_size("chip")
-    blocks = terms.reshape(chips, half // chips, width)
+    blocks = terms.reshape(chips, 8, TILE)
     swapped = lax.all_to_all(blocks, ("group", "chip"), 0, 0, tiled=True)
-    return jnp.sum(swapped, axis=0).T.astype(BF16)
+    columns = pl.pallas_call(
+        sum_kernel,
+        out_shape=jax.ShapeDtypeStruct((half // chips, width), BF16),
+        in_specs=[VMEM],
+        out_specs=VMEM,
+        compiler_params=pltpu.CompilerParams(vmem_limit_bytes=8 * 2**20),
+    )(swapped)
+    return columns.T
 
 
 def solution(mesh):

time: 39.2 us -> 37.3 us (0.952)
  Pallas kernels: 12.7 us -> 11.6 us
  other arithmetic: 0.7 us -> 0 us
    pallas_call x1 -> x2, Pallas kernels: 8.31 us -> 7.27 us  [the longest x1 6.61 us: per_device(): pl.pallas_call(chain_kernel, out_shape=jax.ShapeDtypeStruct((half // 8, 2...]
    reduce_sum x1 -> x0, other arithmetic: 0.7 us -> none  [per_device(): return jnp.sum(swapped, axis=0).T.astype(BF16)]
where the time goes in v3:
time: 37.3 us; the launch traced here: 37.1 us
  blocking collectives  25 us (67%)
  Pallas kernels  11.6 us (31%)
  waiting for transfers between devices  0.44 us (1%)
    all_to_all x1, blocking collectives, per_device(): swapped = lax.all_to_all(blocks, ('group', 'chip'), 0, 0, tiled=True)  25 us
    pallas_call x1, Pallas kernels, per_device(): pl.pallas_call(chain_kernel, out_shape=jax.ShapeDtypeStruct((half // 8, 2...  6.61 us
    pallas_call x1, Pallas kernels, per_device(): pl.pallas_call(send_kernel, out_shape=(summit, jax.ShapeDtypeStruct(matri...  2.9 us
    pallas_call x1, Pallas kernels, per_device(): pl.pallas_call(keep_kernel, out_shape=summit, in_specs=[VMEM] * 3, out_sp...  1.45 us
  transfers between devices with their start and end apart: 1, of which 1 were waited for; matrix products, arithmetic and copies ran while one was open for 0% of the time, Pallas kernels for 4%

profile of v3, /device:TPU:0, one launch (start us, length us, event | category | flops | bytes accessed | tf_op | source)
XLA Modules:
  0.0 37.1 jit_solution(8753141878134425959)
XLA Ops:
  0.0 2.9 %shard_map.73 = (f32[256,512]{1,0:T(8,128)S(1)}, bf16[1024,512]{1,0:T(8,128)(2,1)S(1)}, bf16[1024,512]{1,0:T(8,128)(2,1)S(1)}, bf16[512,512]{1,0:T(8,128)(2,1)S(...) custom-call(bf16[1024,512]{1,0:T(8,128)(2,1)} %x_hbm.1, bf16[1024,512]{1,0:T(8,128)(2,1)} %v_hbm.1, ...), custom_call_target="tpu_custom_call" | custom-call | flops 1073741824 | bytes 4194304 | tf_op jit(solution)/shard_map/pallas_call | solution.py:296
  2.9 0.1 collective-permute-start
  3.0 1.4 %shard_map.74.own_ref = f32[256,512]{1,0:T(8,128)S(1)} custom-call(bf16[1024,512]{1,0:T(8,128)(2,1)S(1)} %get-tuple-element.11.x_ref, bf16[1024,512]{1,0:T(8,128)(2,1)S(1)} %get-tuple-element.12.v_ref, bf16[512,512]{1,0:T(8,128)(2,1)S(1)} %get-tuple-element.13.f_ref), custom_call_target="tpu_custom_call" | custom-call | flops 1073741824 | bytes 4194304 | tf_op jit(solution)/shard_map/pallas_call | solution.py:313
  4.5 0.4 %collective-permute-done.other_ref = f32[256,512]{1,0:T(8,128)S(1)} collective-permute-done((f32[256,512]{1,0:T(8,128)S(1)}, f32[256,512]{1,0:T(8,128)S(1)}, u32[]{:S(2)}, u32[]{:S(2)}) %collective-permute-start) | collective-permute-done | bytes 524320 | tf_op jit(solution)/shard_map/ppermute | solution.py:312
  4.9 6.6 %shard_map.75 = f32[32,2,8,256]{3,2,1,0:T(8,128)S(1)} custom-call(f32[256,512]{1,0:T(8,128)S(1)} %shard_map.74.own_ref, f32[256,512]{1,0:T(8,128)S(1)} %collective-permute-done.other_ref, bf16[2,1024,512]{2,1,0:T(8,128)(2,1)S(1)} %get-tuple-element.15.wv_ref, bf16[2,512,512]{2,1,0:T(8,128)(2,1)S(1)} %get-tuple-element.16.wf_ref, ...), custom_call_target="tpu_custom_call" | custom-call | flops 5905580032 | bytes 12582912 | tf_op jit(solution)/shard_map/pallas_call | solution.py:322
  11.5 25.0 %all_to_all.5.terms_ref = f32[64,8,256]{2,1,0:T(8,128)S(1)} all-to-all(f32[64,8,256]{2,1,0:T(8,128)S(1)} %bitcast.7), channel_id=1, replica_groups=mesh['group'=4,'chip'=16,'core'=2] {'group','chip'}, dimensions={0} | all-to-all | bytes 1048576 | tf_op jit(solution)/shard_map/all_to_all | solution.py:337
  36.5 0.7 %shard_map.76 = bf16[4,512]{1,0:T(4,128)(2,1)} custom-call(f32[64,8,256]{2,1,0:T(8,128)S(1)} %all_to_all.5.terms_ref), custom_call_target="tpu_custom_call" | custom-call | tf_op jit(solution)/shard_map/pallas_call | solution.py:338
Async XLA Ops:
  2.9 2.0 %collective-permute-start = (f32[256,512]{1,0:T(8,128)S(1)}, f32[256,512]{1,0:T(8,128)S(1)}, u32[]{:S(2)}, u32[]{:S(2)}) collective-permute-start(f32[256,512]{1,0:T(8,128)S(1)} %get-tuple-element.14), channel_id=1, source_target_pairs={{0,1},{1,0},{2,3},{3,2},{4,5},{5,4},{6,7},{7,6},{8,9},{9,8},{10,11... | collective-permute-start | bytes 1572872 | tf_op jit(solution)/shard_map/ppermute | solution.py:312

commit v4 on v3

--- a/solution.py
+++ b/solution.py
@@ -7,11 +7,9 @@
 from jax.experimental.pallas import tpu as pltpu
 from jax.sharding import Mesh, PartitionSpec as P
 
-NT = (((1,), (1,)), ((), ()))
-NN = (((1,), (0,)), ((), ()))
 TILE = 256
 UNITS = 2
-GROUPS = 4
+GROUPS = (96, 80, 80)
 F32 = jnp.float32
 BF16 = jnp.bfloat16
 VMEM = pl.BlockSpec(memory_space=pltpu.VMEM)
@@ -43,7 +41,7 @@
 
 
 def run_stages(stages, lhs, sums):
-    groups = len(lhs)
+    groups = len(GROUPS)
     slots = []
     for index, (plan, _, _) in enumerate(stages):
         rounds = max(len(plan(unit)) for unit in range(UNITS))
@@ -74,7 +72,7 @@
             pltpu.matmul_push_rhs(matrix, pushed[unit] % 2, unit, transpose=transpose)
             pushed[unit] += 1
 
-    rows = {(0, group): lhs[group] for group in range(groups)}
+    rows = {}
     waiting = [(index, group) for index in range(len(stages)) for group in range(groups)]
 
     def finish():
@@ -84,7 +82,10 @@
 
     for position, slot in enumerate(slots):
         while slot[:2] not in rows:
-            finish()
+            if slot[0]:
+                finish()
+            else:
+                rows[slot[:2]] = lhs(slot[1])
         for part in range(len(rows[slot[:2]][0])):
             for unit in range(UNITS):
                 depth = depth_of(unit, slot)
@@ -104,16 +105,18 @@
         finish()
 
 
-def with_sums(body, rows):
+def with_sums(body, kinds=1):
     def scoped(*flat):
-        body([flat[unit * GROUPS : (unit + 1) * GROUPS] for unit in range(UNITS)])
+        flat = iter(flat)
+        body(*[[[next(flat) for _ in GROUPS] for _ in range(UNITS)] for _ in range(kinds)])
 
     pl.run_scoped(
         scoped,
         *[
-            pltpu.ACC(unit)((rows // GROUPS, TILE), F32)
+            pltpu.ACC(unit)((count, TILE), F32)
+            for _ in range(kinds)
             for unit in range(UNITS)
-            for _ in range(GROUPS)
+            for count in GROUPS
         ],
     )
 
@@ -125,7 +128,7 @@
 def once(copies):
     done = set()
 
-    def ready(index=0):
+    def ready(index):
         if index not in done:
             done.add(index)
             copies[index].wait()
@@ -143,57 +146,96 @@
     return copies
 
 
-def split_dot(rows, weights, dims):
-    count = rows.shape[0]
-    high = rows.astype(BF16)
-    low = (rows - high.astype(F32)).astype(BF16)
-    both = lax.dot_general(
-        jnp.concatenate([high, low], axis=0), weights, dims, preferred_element_type=F32
-    )
-    return both[:count] + both[count:]
-
-
-def mix_dot(rows, triangle):
-    half = triangle.shape[0] // 2
-    left = split_dot(rows[:, :half], triangle[:half, :half], NN)
-    right = split_dot(rows, triangle[:, half:], NN)
-    return jnp.concatenate([left, right], axis=1)
-
-
-def finish_leaf(top, projected, v_ref, f_ref):
-    mixing = mix_dot(projected, f_ref[...])
-    return top - split_dot(mixing, v_ref[: f_ref.shape[0], :], NT)
+def run_leaf(side, x_ref, v_ref, f_ref, out_ref, ready):
+    blocks = x_ref.shape[0] // TILE
+    offsets = [sum(GROUPS[:group]) for group in range(len(GROUPS))]
+    spans = [slice(start, start + count) for start, count in zip(offsets, GROUPS, strict=True)]
+    pick = pick_rows(side, out_ref.shape[0])
+
+    def body(first, second, sums, late):
+        pushed = [0] * UNITS
+
+        def push(unit, count):
+            while pushed[unit] < min(count, 2 * blocks):
+                load = pushed[unit]
+                if load < blocks:
+                    out, depth = UNITS * (load // 2) + unit, load % 2
+                    ready(out)
+                    matrix = x_ref[tile(out), tile(depth)]
+                else:
+                    ready(load)
+                    matrix = v_ref[tile(load - blocks), tile(unit)]
+                pltpu.matmul_push_rhs(matrix, load % 2, unit, transpose=load < blocks)
+                pushed[unit] += 1
+
+        def product(load, totals, rows):
+            for unit in range(UNITS):
+                push(unit, load + 1)
+                for group, part in enumerate(rows):
+                    pltpu.matmul_acc_lhs(
+                        totals[unit][group], part, load_staged_rhs=None if group else load % 2
+                    )
+                push(unit, load + 2)
+
+        for load in range(blocks):
+            totals = first if load < 2 else second
+            product(load, totals, [pick[span, tile(load % 2)] for span in spans])
+        tops = []
+        for index, totals in enumerate((first, second)):
+            panel = [
+                [pltpu.matmul_pop(totals[unit][group]) for group in range(len(GROUPS))]
+                for unit in range(UNITS)
+            ]
+            if index == 0:
+                tops = panel
+            for unit in range(UNITS):
+                rows = [values.astype(BF16) for values in panel[unit]]
+                product(blocks + UNITS * index + unit, sums, rows)
+
+        def projected(group):
+            return pairs(group, [pltpu.matmul_pop(sums[unit][group]) for unit in range(UNITS)])
+
+        def triangle(out, depth):
+            ready(2 * blocks)
+            return f_ref[tile(depth), tile(out)], False
+
+        def top(out, depth):
+            return v_ref[tile(out), tile(depth)], True
+
+        def finish(group, tiles):
+            for out, values in enumerate(tiles):
+                out_ref[pl.ds(offsets[group], GROUPS[group]), tile(out)] = tops[out][group] - values
+
+        run_stages(
+            [(triangle_plan, triangle, pairs), (by_columns(2), top, finish)], projected, late
+        )
+
+    with_sums(body, 4)
 
 
 def send_kernel(x_hbm, v_hbm, f_hbm, ib_hbm, it_hbm, out_ref, x_ref, v_ref, f_ref, wv_ref, wf_ref, sems):
-    sources, targets = [x_hbm, v_hbm, f_hbm], [x_ref, v_ref, f_ref]
+    tiles = [pl.ds(block * TILE, TILE) for block in range(x_hbm.shape[0] // TILE)]
+    sources = [ref.at[span] for ref in (x_hbm, v_hbm) for span in tiles] + [f_hbm]
+    targets = [ref.at[span] for ref in (x_ref, v_ref) for span in tiles] + [f_ref]
     for level in range(wv_ref.shape[0]):
         sources += [ib_hbm.at[level], it_hbm.at[level]]
         targets += [wv_ref.at[level], wf_ref.at[level]]
     copies = fetch(sources, targets, sems)
-    pick = pick_rows(1 - lax.axis_index("core"), out_ref.shape[0])
-    copies[0].wait()
-    panel = lax.dot_general(pick, x_ref[...], NT, preferred_element_type=F32)
-    copies[1].wait()
-    copies[2].wait()
-    projected = lax.dot_general(panel.astype(BF16), v_ref[...], NN, preferred_element_type=F32)
-    out_ref[...] = finish_leaf(panel[:, : f_ref.shape[0]], projected, v_ref, f_ref)
-    for copy in copies[3:]:
+    side = 1 - lax.axis_index("core")
+    run_leaf(side, x_ref, v_ref, f_ref, out_ref, once(copies))
+    for copy in copies[2 * len(tiles) + 1 :]:
         copy.wait()
 
 
 def keep_kernel(x_ref, v_ref, f_ref, out_ref):
-    pick = pick_rows(lax.axis_index("core"), out_ref.shape[0])
-    panel = lax.dot_general(pick, x_ref[...], NT, preferred_element_type=F32)
-    projected = lax.dot_general(panel.astype(BF16), v_ref[...], NN, preferred_element_type=F32)
-    out_ref[...] = finish_leaf(panel[:, : f_ref.shape[0]], projected, v_ref, f_ref)
+    run_leaf(lax.axis_index("core"), x_ref, v_ref, f_ref, out_ref, lambda index: None)
 
 
 def chain_kernel(
     own_ref, other_ref, wv_ref, wf_ref, ib_hbm, it_hbm, ob_hbm, ot_hbm, out_ref, v_buf, f_buf, sems
 ):
-    rows, width = own_ref.shape
-    count = rows // GROUPS
+    width = own_ref.shape[1]
+    offsets = [sum(GROUPS[:group]) for group in range(len(GROUPS))]
     early, inner, outer = wv_ref.shape[0], ib_hbm.shape[0], ob_hbm.shape[0]
     sources = []
     for level in range(early, inner):
@@ -205,7 +247,7 @@
     arrived = once(fetch(sources, targets, sems))
     core = lax.axis_index("core")
     place = lax.axis_index("group") * lax.axis_size("chip") + lax.axis_index("chip")
-    summit = [None] * GROUPS
+    summit = [None] * len(GROUPS)
 
     def level_stages(level):
         basis_ref, tri_ref, at = (
@@ -238,11 +280,12 @@
         def last(group, tiles):
             after(group, tiles)
             left, right = summit[group]
+            count = GROUPS[group]
             upper = lax.broadcasted_iota(jnp.int32, (count, TILE), 0) % 8 < 4
             even = jnp.where(upper, left, pltpu.roll(right, 4, 0))
             odd = jnp.where(upper, pltpu.roll(left, count - 4, 0), right)
             for index, values in enumerate((even, odd)):
-                at = pl.ds(group * count // 8, count // 8)
+                at = pl.ds(offsets[group] // 8, count // 8)
                 out_ref[at, index] = values.reshape(count // 8, 8, TILE)
 
         end = last if level == inner + outer - 1 else after
@@ -252,16 +295,16 @@
             (by_columns(2), top, end),
         ]
 
-    lhs = []
-    for group in range(GROUPS):
-        at = pl.ds(group * count, count)
+    def lhs(group):
+        at = pl.ds(offsets[group], GROUPS[group])
         own = [own_ref[at, tile(out)] for out in range(2)]
         other = [other_ref[at, tile(out)] for out in range(2)]
         summit[group] = [jnp.where(core == 0, a, b) for a, b in zip(own, other, strict=True)]
         upper = [jnp.where(core == 0, b, a) for a, b in zip(own, other, strict=True)]
-        lhs.append(pairs(group, summit[group] + upper))
+        return pairs(group, summit[group] + upper)
+
     stages = [stage for level in range(inner + outer) for stage in level_stages(level)]
-    with_sums(lambda sums: run_stages(stages, lhs, sums), rows)
+    with_sums(lambda sums: run_stages(stages, lhs, sums))
 
 
 def in_hbm(array):
@@ -305,7 +348,7 @@
         ),
         in_specs=[HBM] * 5,
         out_specs=(VMEM,) * 6,
-        scratch_shapes=[pltpu.SemaphoreType.DMA((3 + 2 * ahead,))],
+        scratch_shapes=[pltpu.SemaphoreType.DMA((2 * rows // TILE + 1 + 2 * ahead,))],
         cost_estimate=estimate(4, 4),
         compiler_params=pltpu.CompilerParams(vmem_limit_bytes=16 * 2**20),
     )(in_hbm(matrix), in_hbm(leaf_basis), in_hbm(leaf_tri[0]), *trees)

time: 37.3 us -> 37.1 us (level)
  no operation moved by 1% of the time
where the time goes in v4:
time: 37.1 us; the launch traced here: 36.9 us
  blocking collectives  25 us (67%)
  Pallas kernels  11.3 us (30%)
  waiting for transfers between devices  0.49 us (1%)
    all_to_all x1, blocking collectives, per_device(): swapped = lax.all_to_all(blocks, ('group', 'chip'), 0, 0, tiled=True)  25 us
    pallas_call x1, Pallas kernels, per_device(): pl.pallas_call(chain_kernel, out_shape=jax.ShapeDtypeStruct((half // 8, 2...  6.45 us
    pallas_call x1, Pallas kernels, per_device(): pl.pallas_call(send_kernel, out_shape=(summit, jax.ShapeDtypeStruct(matri...  2.83 us
    pallas_call x1, Pallas kernels, per_device(): pl.pallas_call(keep_kernel, out_shape=summit, in_specs=[VMEM] * 3, out_sp...  1.4 us
  transfers between devices with their start and end apart: 1, of which 1 were waited for; matrix products, arithmetic and copies ran while one was open for 0% of the time, Pallas kernels for 4%

profile of v4, /device:TPU:0, one launch (start us, length us, event | category | flops | bytes accessed | tf_op | source)
XLA Modules:
  0.0 36.9 jit_solution(1850469240895851801)
XLA Ops:
  0.0 2.8 %shard_map.73 = (f32[256,512]{1,0:T(8,128)S(1)}, bf16[1024,512]{1,0:T(8,128)(2,1)S(1)}, bf16[1024,512]{1,0:T(8,128)(2,1)S(1)}, bf16[512,512]{1,0:T(8,128)(2,1)S(...) custom-call(bf16[1024,512]{1,0:T(8,128)(2,1)} %x_hbm.1, bf16[1024,512]{1,0:T(8,128)(2,1)} %v_hbm.1, ...), custom_call_target="tpu_custom_call" | custom-call | flops 1073741824 | bytes 4194304 | tf_op jit(solution)/shard_map/pallas_call | solution.py:339
  2.8 0.1 collective-permute-start
  2.9 1.4 %shard_map.74.own_ref = f32[256,512]{1,0:T(8,128)S(1)} custom-call(bf16[1024,512]{1,0:T(8,128)(2,1)S(1)} %get-tuple-element.11.x_ref, bf16[1024,512]{1,0:T(8,128)(2,1)S(1)} %get-tuple-element.12.v_ref, bf16[512,512]{1,0:T(8,128)(2,1)S(1)} %get-tuple-element.13.f_ref), custom_call_target="tpu_custom_call" | custom-call | flops 1073741824 | bytes 4194304 | tf_op jit(solution)/shard_map/pallas_call | solution.py:356
  4.3 0.5 %collective-permute-done.other_ref = f32[256,512]{1,0:T(8,128)S(1)} collective-permute-done((f32[256,512]{1,0:T(8,128)S(1)}, f32[256,512]{1,0:T(8,128)S(1)}, u32[]{:S(2)}, u32[]{:S(2)}) %collective-permute-start) | collective-permute-done | bytes 524320 | tf_op jit(solution)/shard_map/ppermute | solution.py:355
  4.8 6.4 %shard_map.75 = f32[32,2,8,256]{3,2,1,0:T(8,128)S(1)} custom-call(f32[256,512]{1,0:T(8,128)S(1)} %shard_map.74.own_ref, f32[256,512]{1,0:T(8,128)S(1)} %collective-permute-done.other_ref, bf16[2,1024,512]{2,1,0:T(8,128)(2,1)S(1)} %get-tuple-element.15.wv_ref, bf16[2,512,512]{2,1,0:T(8,128)(2,1)S(1)} %get-tuple-element.16.wf_ref, ...), custom_call_target="tpu_custom_call" | custom-call | flops 5905580032 | bytes 12582912 | tf_op jit(solution)/shard_map/pallas_call | solution.py:365
  11.3 25.0 %all_to_all.5.terms_ref = f32[64,8,256]{2,1,0:T(8,128)S(1)} all-to-all(f32[64,8,256]{2,1,0:T(8,128)S(1)} %bitcast.7), channel_id=1, replica_groups=mesh['group'=4,'chip'=16,'core'=2] {'group','chip'}, dimensions={0} | all-to-all | bytes 1048576 | tf_op jit(solution)/shard_map/all_to_all | solution.py:380
  36.3 0.7 %shard_map.76 = bf16[4,512]{1,0:T(4,128)(2,1)} custom-call(f32[64,8,256]{2,1,0:T(8,128)S(1)} %all_to_all.5.terms_ref), custom_call_target="tpu_custom_call" | custom-call | tf_op jit(solution)/shard_map/pallas_call | solution.py:381
Async XLA Ops:
  2.8 2.0 %collective-permute-start = (f32[256,512]{1,0:T(8,128)S(1)}, f32[256,512]{1,0:T(8,128)S(1)}, u32[]{:S(2)}, u32[]{:S(2)}) collective-permute-start(f32[256,512]{1,0:T(8,128)S(1)} %get-tuple-element.14), channel_id=1, source_target_pairs={{0,1},{1,0},{2,3},{3,2},{4,5},{5,4},{6,7},{7,6},{8,9},{9,8},{10,11... | collective-permute-start | bytes 1572872 | tf_op jit(solution)/shard_map/ppermute | solution.py:355

commit v5 on v4

--- a/solution.py
+++ b/solution.py
@@ -33,23 +33,30 @@
 
 
 def by_columns(depth):
-    return lambda unit: range(depth)
-
-
-def triangle_plan(unit):
-    return range(unit + 1)
-
-
-def run_stages(stages, lhs, sums):
+    return lambda unit, group: [(unit, block) for block in range(depth)]
+
+
+def triangle_plan(unit, group):
+    return [(unit, block) for block in range(unit + 1)]
+
+
+def even_triangle_plan(unit, group):
+    if group == 1:
+        return [(0, 0), (1, 0), (1, 1)] if unit == 0 else []
+    return [(0, 0)] if unit == 0 else [(1, 0), (1, 1)]
+
+
+def run_stages(stages, lhs, sums, spare):
     groups = len(GROUPS)
     slots = []
     for index, (plan, _, _) in enumerate(stages):
-        rounds = max(len(plan(unit)) for unit in range(UNITS))
-        slots += [(index, group, at) for group in range(groups) for at in range(rounds)]
+        for group in range(groups):
+            rounds = max(len(plan(unit, group)) for unit in range(UNITS))
+            slots += [(index, group, at) for at in range(rounds)]
 
     def depth_of(unit, slot):
         index, group, at = slot
-        order = list(stages[index][0](unit))
+        order = stages[index][0](unit, group)
         order = order[::-1] if group % 2 else order
         return order[at] if at < len(order) else None
 
@@ -67,18 +74,27 @@
 
     def push(unit, count):
         while pushed[unit] < min(count, len(loads[unit])):
-            index, depth = loads[unit][pushed[unit]]
-            matrix, transpose = stages[index][1](unit, depth)
+            index, product = loads[unit][pushed[unit]]
+            matrix, transpose = stages[index][1](*product)
             pltpu.matmul_push_rhs(matrix, pushed[unit] % 2, unit, transpose=transpose)
             pushed[unit] += 1
 
+    def outs_of(index, unit, group):
+        return sorted({product[0] for product in stages[index][0](unit, group)})
+
+    def total_of(index, unit, group, out):
+        return (sums, spare)[outs_of(index, unit, group).index(out)][unit][group]
+
     rows = {}
     waiting = [(index, group) for index in range(len(stages)) for group in range(groups)]
 
     def finish():
         index, group = waiting.pop(0)
-        tiles = [pltpu.matmul_pop(sums[unit][group]) for unit in range(UNITS)]
-        rows[index + 1, group] = stages[index][2](group, tiles)
+        tiles = {}
+        for unit in range(UNITS):
+            for out in outs_of(index, unit, group):
+                tiles[out] = pltpu.matmul_pop(total_of(index, unit, group, out))
+        rows[index + 1, group] = stages[index][2](group, [tiles[out] for out in sorted(tiles)])
 
     for position, slot in enumerate(slots):
         while slot[:2] not in rows:
@@ -95,8 +111,8 @@
                 if load is not None:
                     push(unit, load + 1)
                 pltpu.matmul_acc_lhs(
-                    sums[unit][slot[1]],
-                    rows[slot[:2]][depth][part],
+                    total_of(*slot[:1], unit, slot[1], depth[0]),
+                    rows[slot[:2]][depth[1]][part],
                     load_staged_rhs=None if load is None else load % 2,
                 )
                 if load is not None:
@@ -207,7 +223,7 @@
                 out_ref[pl.ds(offsets[group], GROUPS[group]), tile(out)] = tops[out][group] - values
 
         run_stages(
-            [(triangle_plan, triangle, pairs), (by_columns(2), top, finish)], projected, late
+            [(even_triangle_plan, triangle, pairs), (by_columns(2), top, finish)], projected, late, first
         )
 
     with_sums(body, 4)
@@ -304,7 +320,7 @@
         return pairs(group, summit[group] + upper)
 
     stages = [stage for level in range(inner + outer) for stage in level_stages(level)]
-    with_sums(lambda sums: run_stages(stages, lhs, sums))
+    with_sums(lambda sums, spare: run_stages(stages, lhs, sums, spare), 2)
 
 
 def in_hbm(array):

time: 37.1 us -> 37 us (level)
  no operation moved by 1% of the time
where the time goes in v5:
time: 37 us; the launch traced here: 36.9 us
  blocking collectives  25 us (68%)
  Pallas kernels  11.2 us (30%)
  waiting for transfers between devices  0.54 us (1%)
    all_to_all x1, blocking collectives, per_device(): swapped = lax.all_to_all(blocks, ('group', 'chip'), 0, 0, tiled=True)  25 us
    pallas_call x1, Pallas kernels, per_device(): pl.pallas_call(chain_kernel, out_shape=jax.ShapeDtypeStruct((half // 8, 2...  6.45 us
    pallas_call x1, Pallas kernels, per_device(): pl.pallas_call(send_kernel, out_shape=(summit, jax.ShapeDtypeStruct(matri...  2.77 us
    pallas_call x1, Pallas kernels, per_device(): pl.pallas_call(keep_kernel, out_shape=summit, in_specs=[VMEM] * 3, out_sp...  1.35 us
  transfers between devices with their start and end apart: 1, of which 1 were waited for; matrix products, arithmetic and copies ran while one was open for 0% of the time, Pallas kernels for 4%

profile of v5, /device:TPU:0, one launch (start us, length us, event | category | flops | bytes accessed | tf_op | source)
XLA Modules:
  0.0 36.9 jit_solution(18395726438367161363)
XLA Ops:
  0.0 2.8 %shard_map.73 = (f32[256,512]{1,0:T(8,128)S(1)}, bf16[1024,512]{1,0:T(8,128)(2,1)S(1)}, bf16[1024,512]{1,0:T(8,128)(2,1)S(1)}, bf16[512,512]{1,0:T(8,128)(2,1)S(...) custom-call(bf16[1024,512]{1,0:T(8,128)(2,1)} %x_hbm.1, bf16[1024,512]{1,0:T(8,128)(2,1)} %v_hbm.1, ...), custom_call_target="tpu_custom_call" | custom-call | flops 1073741824 | bytes 4194304 | tf_op jit(solution)/shard_map/pallas_call | solution.py:355
  2.8 0.1 collective-permute-start
  2.9 1.4 %shard_map.74.own_ref = f32[256,512]{1,0:T(8,128)S(1)} custom-call(bf16[1024,512]{1,0:T(8,128)(2,1)S(1)} %get-tuple-element.11.x_ref, bf16[1024,512]{1,0:T(8,128)(2,1)S(1)} %get-tuple-element.12.v_ref, bf16[512,512]{1,0:T(8,128)(2,1)S(1)} %get-tuple-element.13.f_ref), custom_call_target="tpu_custom_call" | custom-call | flops 1073741824 | bytes 4194304 | tf_op jit(solution)/shard_map/pallas_call | solution.py:372
  4.2 0.5 %collective-permute-done.other_ref = f32[256,512]{1,0:T(8,128)S(1)} collective-permute-done((f32[256,512]{1,0:T(8,128)S(1)}, f32[256,512]{1,0:T(8,128)S(1)}, u32[]{:S(2)}, u32[]{:S(2)}) %collective-permute-start) | collective-permute-done | bytes 524320 | tf_op jit(solution)/shard_map/ppermute | solution.py:371
  4.8 6.4 %shard_map.75 = f32[32,2,8,256]{3,2,1,0:T(8,128)S(1)} custom-call(f32[256,512]{1,0:T(8,128)S(1)} %shard_map.74.own_ref, f32[256,512]{1,0:T(8,128)S(1)} %collective-permute-done.other_ref, bf16[2,1024,512]{2,1,0:T(8,128)(2,1)S(1)} %get-tuple-element.15.wv_ref, bf16[2,512,512]{2,1,0:T(8,128)(2,1)S(1)} %get-tuple-element.16.wf_ref, ...), custom_call_target="tpu_custom_call" | custom-call | flops 5905580032 | bytes 12582912 | tf_op jit(solution)/shard_map/pallas_call | solution.py:381
  11.2 25.0 %all_to_all.5.terms_ref = f32[64,8,256]{2,1,0:T(8,128)S(1)} all-to-all(f32[64,8,256]{2,1,0:T(8,128)S(1)} %bitcast.7), channel_id=1, replica_groups=mesh['group'=4,'chip'=16,'core'=2] {'group','chip'}, dimensions={0} | all-to-all | bytes 1048576 | tf_op jit(solution)/shard_map/all_to_all | solution.py:396
  36.2 0.7 %shard_map.76 = bf16[4,512]{1,0:T(4,128)(2,1)} custom-call(f32[64,8,256]{2,1,0:T(8,128)S(1)} %all_to_all.5.terms_ref), custom_call_target="tpu_custom_call" | custom-call | tf_op jit(solution)/shard_map/pallas_call | solution.py:397
Async XLA Ops:
  2.8 2.0 %collective-permute-start = (f32[256,512]{1,0:T(8,128)S(1)}, f32[256,512]{1,0:T(8,128)S(1)}, u32[]{:S(2)}, u32[]{:S(2)}) collective-permute-start(f32[256,512]{1,0:T(8,128)S(1)} %get-tuple-element.14), channel_id=1, source_target_pairs={{0,1},{1,0},{2,3},{3,2},{4,5},{5,4},{6,7},{7,6},{8,9},{9,8},{10,11... | collective-permute-start | bytes 1572872 | tf_op jit(solution)/shard_map/ppermute | solution.py:371

commit v6 on v5

--- a/solution.py
+++ b/solution.py
@@ -9,7 +9,7 @@
 
 TILE = 256
 UNITS = 2
-GROUPS = (96, 80, 80)
+GROUPS = (80, 80, 96)
 F32 = jnp.float32
 BF16 = jnp.bfloat16
 VMEM = pl.BlockSpec(memory_space=pltpu.VMEM)

time: 37 us -> 37 us (level)
  no operation moved by 1% of the time
where the time goes in v6:
time: 37 us; the launch traced here: 36.8 us
  blocking collectives  25 us (68%)
  Pallas kernels  11.2 us (30%)
  waiting for transfers between devices  0.54 us (1%)
    all_to_all x1, blocking collectives, per_device(): swapped = lax.all_to_all(blocks, ('group', 'chip'), 0, 0, tiled=True)  25 us
    pallas_call x1, Pallas kernels, per_device(): pl.pallas_call(chain_kernel, out_shape=jax.ShapeDtypeStruct((half // 8, 2...  6.42 us
    pallas_call x1, Pallas kernels, per_device(): pl.pallas_call(send_kernel, out_shape=(summit, jax.ShapeDtypeStruct(matri...  2.77 us
    pallas_call x1, Pallas kernels, per_device(): pl.pallas_call(keep_kernel, out_shape=summit, in_specs=[VMEM] * 3, out_sp...  1.35 us
  transfers between devices with their start and end apart: 1, of which 1 were waited for; matrix products, arithmetic and copies ran while one was open for 0% of the time, Pallas kernels for 4%

profile of v6, /device:TPU:0, one launch (start us, length us, event | category | flops | bytes accessed | tf_op | source)
XLA Modules:
  0.0 36.8 jit_solution(12818143491091719169)
XLA Ops:
  0.0 2.8 %shard_map.73 = (f32[256,512]{1,0:T(8,128)S(1)}, bf16[1024,512]{1,0:T(8,128)(2,1)S(1)}, bf16[1024,512]{1,0:T(8,128)(2,1)S(1)}, bf16[512,512]{1,0:T(8,128)(2,1)S(...) custom-call(bf16[1024,512]{1,0:T(8,128)(2,1)} %x_hbm.1, bf16[1024,512]{1,0:T(8,128)(2,1)} %v_hbm.1, ...), custom_call_target="tpu_custom_call" | custom-call | flops 1073741824 | bytes 4194304 | tf_op jit(solution)/shard_map/pallas_call | solution.py:355
  2.8 0.1 collective-permute-start
  2.9 1.3 %shard_map.74.own_ref = f32[256,512]{1,0:T(8,128)S(1)} custom-call(bf16[1024,512]{1,0:T(8,128)(2,1)S(1)} %get-tuple-element.11.x_ref, bf16[1024,512]{1,0:T(8,128)(2,1)S(1)} %get-tuple-element.12.v_ref, bf16[512,512]{1,0:T(8,128)(2,1)S(1)} %get-tuple-element.13.f_ref), custom_call_target="tpu_custom_call" | custom-call | flops 1073741824 | bytes 4194304 | tf_op jit(solution)/shard_map/pallas_call | solution.py:372
  4.2 0.5 %collective-permute-done.other_ref = f32[256,512]{1,0:T(8,128)S(1)} collective-permute-done((f32[256,512]{1,0:T(8,128)S(1)}, f32[256,512]{1,0:T(8,128)S(1)}, u32[]{:S(2)}, u32[]{:S(2)}) %collective-permute-start) | collective-permute-done | bytes 524320 | tf_op jit(solution)/shard_map/ppermute | solution.py:371
  4.8 6.4 %shard_map.75 = f32[32,2,8,256]{3,2,1,0:T(8,128)S(1)} custom-call(f32[256,512]{1,0:T(8,128)S(1)} %shard_map.74.own_ref, f32[256,512]{1,0:T(8,128)S(1)} %collective-permute-done.other_ref, bf16[2,1024,512]{2,1,0:T(8,128)(2,1)S(1)} %get-tuple-element.15.wv_ref, bf16[2,512,512]{2,1,0:T(8,128)(2,1)S(1)} %get-tuple-element.16.wf_ref, ...), custom_call_target="tpu_custom_call" | custom-call | flops 5905580032 | bytes 12582912 | tf_op jit(solution)/shard_map/pallas_call | solution.py:381
  11.2 25.0 %all_to_all.5.terms_ref = f32[64,8,256]{2,1,0:T(8,128)S(1)} all-to-all(f32[64,8,256]{2,1,0:T(8,128)S(1)} %bitcast.7), channel_id=1, replica_groups=mesh['group'=4,'chip'=16,'core'=2] {'group','chip'}, dimensions={0} | all-to-all | bytes 1048576 | tf_op jit(solution)/shard_map/all_to_all | solution.py:396
  36.2 0.7 %shard_map.76 = bf16[4,512]{1,0:T(4,128)(2,1)} custom-call(f32[64,8,256]{2,1,0:T(8,128)S(1)} %all_to_all.5.terms_ref), custom_call_target="tpu_custom_call" | custom-call | tf_op jit(solution)/shard_map/pallas_call | solution.py:397
Async XLA Ops:
  2.8 2.0 %collective-permute-start = (f32[256,512]{1,0:T(8,128)S(1)}, f32[256,512]{1,0:T(8,128)S(1)}, u32[]{:S(2)}, u32[]{:S(2)}) collective-permute-start(f32[256,512]{1,0:T(8,128)S(1)} %get-tuple-element.14), channel_id=1, source_target_pairs={{0,1},{1,0},{2,3},{3,2},{4,5},{5,4},{6,7},{7,6},{8,9},{9,8},{10,11... | collective-permute-start | bytes 1572872 | tf_op jit(solution)/shard_map/ppermute | solution.py:371
